TPU v7x, 32 devices: a whole 2x2x4 slice. The times are simulated.
32 devices in a mesh: seq: 4 (over y, x), dp: 8 (over z, core).
Axes of the slice: x: 2, y: 2, z: 4, core: 2. Of those that a mesh axis runs over, the one named last changes fastest.
Arguments:
- layer_input: bfloat16 [8, 1024, 8192], P('dp', 'seq'), may hold values from -400 to 400
- frozen_queries: bfloat16 [8, 1024, 6144], P('dp', 'seq'), may hold values from -70 to 70
- frozen_keys: bfloat16 [8, 1024, 768], P('dp', 'seq'), may hold values from -6 to 6
- frozen_values: bfloat16 [8, 1024, 768], P('dp', 'seq'), may hold values from -6 to 6
- output_gradient: bfloat16 [8, 1024, 6144], P('dp', 'seq'), may hold values from -6 to 6
- norm_scale_vector: bfloat16 [8192], replicated, may hold values from 0.5 to 1.5
- query_down_weight: bfloat16 [8, 8192], replicated, may hold values from -0.0625 to 0.0625
- query_up_weight: bfloat16 [8, 6144], replicated, may hold values from -2 to 2
- value_down_weight: bfloat16 [8, 8192], replicated, may hold values from -0.0625 to 0.0625
- value_up_weight: bfloat16 [8, 768], replicated, may hold values from -2 to 2
- head_ordering: int32 [6], replicated, may hold values from 0 to 5, each once
Outputs:
- grad_query_a: float32 [8, 8192], replicated
- grad_query_b: float32 [8, 6144], replicated
- grad_value_a: float32 [8, 8192], replicated
- grad_value_b: float32 [8, 768], replicated
- grad_gain: float32 [8192], replicated
Inputs may be any that keep to these rules, and one draw needn't show every extreme that they name: `head_ordering`: a permutation of the 6 key-value heads.
All inputs are finite; a program needn't handle non-finite values.
Results may differ from a plain program's by a relative error of at most 0.012.
The roundings to bfloat16 on the way count: a program that leaves them out, or rounds other values in their place, can miss the bound.
Values may be sent and summed in bfloat16 or wider, within the bound.
A program may use at most 128 MiB of HBM per device.

v0:
```python
import math

import jax
import jax.numpy as jnp
from jax import lax
from jax.sharding import PartitionSpec as P

HEAD_SIZE = 128


EPS = 1e-05
ADAPTER_SCALE = 2.0


def from_behind(block, axis, distance):
    devices = range(lax.axis_size(axis))
    route = [((i - distance) % len(devices), i) for i in devices]
    return lax.ppermute(block, axis, route)


def attend(query_rows, key_rows, values, grad_out, allowed):
    factor = 1.0 / math.sqrt(query_rows.shape[-1])
    scores = (
        jnp.einsum("tgd,ud->gtu", query_rows, key_rows, preferred_element_type=jnp.float32) * factor
    )
    scores = jnp.where(allowed[None], scores, -jnp.inf)
    row_max = jnp.max(scores, axis=-1, keepdims=True)
    exponent = jnp.exp(scores - row_max)
    probs_full = exponent / jnp.sum(exponent, axis=-1, keepdims=True)
    weights = probs_full.astype(jnp.bfloat16)
    attended = jnp.einsum("gtu,ud->tgd", weights, values, preferred_element_type=jnp.float32)
    delta = jnp.sum(grad_out.astype(jnp.float32) * attended, axis=-1)
    dprob = jnp.einsum("tgd,ud->gtu", grad_out, values, preferred_element_type=jnp.float32)
    dscore = (probs_full * (dprob - delta.T[:, :, None])).astype(jnp.bfloat16)
    query_gradient = (
        jnp.einsum("gtu,ud->tgd", dscore, key_rows, preferred_element_type=jnp.float32) * factor
    )
    value_gradient = jnp.einsum(
        "gtu,tgd->ud", weights, grad_out, preferred_element_type=jnp.float32
    )
    return (query_gradient, value_gradient)


def attend_heads(operands):
    return attend(*operands)


def all_heads(query4, keys3, values3, grads4, allowed3):
    operands = (
        jnp.moveaxis(query4, 1, 0),
        jnp.moveaxis(keys3, 1, 0),
        jnp.moveaxis(values3, 1, 0),
        jnp.moveaxis(grads4, 1, 0),
        allowed3,
    )
    query_gradient, value_gradient = lax.map(attend_heads, operands)
    return (jnp.moveaxis(query_gradient, 0, 1), jnp.moveaxis(value_gradient, 0, 1))


def contracted_rows(left, right):
    return lax.dot_general(
        left, right, (((0,), (0,)), ((), ())), preferred_element_type=jnp.float32
    )


def contracted_columns(left, right):
    return lax.dot_general(
        left, right, (((1,), (1,)), ((), ())), preferred_element_type=jnp.float32
    )


def squares_of(parts):
    total = jnp.zeros((), jnp.float32)
    for part in parts:
        total = total + jnp.sum(part * part)
    return total


def shards(
    layer_input,
    frozen_queries,
    frozen_keys,
    frozen_values,
    output_gradient,
    norm_scale_vector,
    query_down_weight,
    query_up_weight,
    value_down_weight,
    value_up_weight,
    head_ordering,
):
    tok_rows = layer_input.shape[1]
    kv_heads = frozen_keys.shape[2] // HEAD_SIZE
    group_size = frozen_queries.shape[2] // frozen_keys.shape[2]
    hidden_f = layer_input[0].astype(jnp.float32)
    inverse = lax.rsqrt(jnp.mean(hidden_f * hidden_f, axis=-1, keepdims=True) + EPS)
    unit = hidden_f * inverse
    normalized_input = (unit * norm_scale_vector.astype(jnp.float32)).astype(jnp.bfloat16)
    query_inner = contracted_columns(normalized_input, query_down_weight).astype(jnp.bfloat16)
    value_inner = contracted_columns(normalized_input, value_down_weight).astype(jnp.bfloat16)
    query_rows = (
        frozen_queries[0].astype(jnp.float32)
        + ADAPTER_SCALE * jnp.dot(query_inner, query_up_weight, preferred_element_type=jnp.float32)
    ).astype(jnp.bfloat16)
    value_rows = (
        frozen_values[0].astype(jnp.float32)
        + ADAPTER_SCALE * jnp.dot(value_inner, value_up_weight, preferred_element_type=jnp.float32)
    ).astype(jnp.bfloat16)
    query4 = query_rows.reshape(tok_rows, kv_heads, group_size, HEAD_SIZE)
    keys3 = frozen_keys[0].reshape(tok_rows, kv_heads, HEAD_SIZE)
    values3 = value_rows.reshape(tok_rows, kv_heads, HEAD_SIZE)
    grads4 = output_gradient[0].reshape(tok_rows, kv_heads, group_size, HEAD_SIZE)
    head_ids = jnp.arange(kv_heads, dtype=jnp.int32)
    moved_ids = head_ordering[: kv_heads // 2]
    displaced_mask = jnp.any(moved_ids[:, None] == head_ids[None, :], axis=0)
    odd_place = lax.axis_index("seq") % 2 == 1
    needs_prior = jnp.logical_xor(displaced_mask, odd_place)
    prior = from_behind((keys3, values3), "seq", 1)
    prior_keys = prior[0]
    prior_values = prior[1]
    keys_ext = jnp.concatenate([prior_keys, keys3], axis=0)
    values_ext = jnp.concatenate([prior_values, values3], axis=0)
    query_pos = jnp.arange(tok_rows)[:, None]
    key_pos = jnp.arange(2 * tok_rows)[None, :]
    own_keys = (key_pos >= tok_rows) & (key_pos - tok_rows <= query_pos)
    prior_keys_mask = key_pos < tok_rows
    allowed3 = own_keys[None] | prior_keys_mask[None] & needs_prior[:, None, None]
    dq_full, dv_ext = all_heads(query4, keys_ext, values_ext, grads4, allowed3)
    handed = from_behind(dv_ext[:tok_rows].astype(jnp.bfloat16), "seq", -1).astype(jnp.float32)
    query_gradient = dq_full.astype(jnp.bfloat16)
    value_gradient = (dv_ext[tok_rows:] + handed).astype(jnp.bfloat16)
    query_gradient_rows = query_gradient.reshape(tok_rows, frozen_queries.shape[2])
    value_gradient_rows = value_gradient.reshape(tok_rows, frozen_keys.shape[2])
    query_up_unscaled = ADAPTER_SCALE * contracted_rows(query_inner, query_gradient_rows)
    value_up_unscaled = ADAPTER_SCALE * contracted_rows(value_inner, value_gradient_rows)
    query_gradient_inner = (
        ADAPTER_SCALE * contracted_columns(query_gradient_rows, query_up_weight)
    ).astype(jnp.bfloat16)
    value_gradient_inner = (
        ADAPTER_SCALE * contracted_columns(value_gradient_rows, value_up_weight)
    ).astype(jnp.bfloat16)
    raw_qa = contracted_rows(query_gradient_inner, normalized_input)
    raw_va = contracted_rows(value_gradient_inner, normalized_input)
    normalized_gradient = jnp.dot(
        query_gradient_inner, query_down_weight, preferred_element_type=jnp.float32
    ) + jnp.dot(value_gradient_inner, value_down_weight, preferred_element_type=jnp.float32)
    raw_gain = jnp.sum(normalized_gradient * unit, axis=0)
    listed_items = (
        query_down_weight.shape[0]
        * (
            query_down_weight.shape[1]
            + query_up_weight.shape[1]
            + value_down_weight.shape[1]
            + value_up_weight.shape[1]
        )
        + norm_scale_vector.shape[0]
    )
    limit = math.sqrt(listed_items)
    summed = lax.psum(
        (raw_qa, query_up_unscaled, raw_va, value_up_unscaled, raw_gain), ("seq", "dp")
    )
    factor = jnp.minimum(1.0, limit / jnp.sqrt(squares_of(summed)))
    return (
        summed[0] * factor,
        summed[1] * factor,
        summed[2] * factor,
        summed[3] * factor,
        summed[4] * factor,
    )


def solution(mesh):
    placed = (
        P("dp", "seq", None),
        P("dp", "seq", None),
        P("dp", "seq", None),
        P("dp", "seq", None),
        P("dp", "seq", None),
        P(),
        P(),
        P(),
        P(),
        P(),
        P(),
    )
    return jax.shard_map(
        shards, mesh=mesh, in_specs=placed, out_specs=(P(), P(), P(), P(), P()), check_vma=False
    )
```

profile of v0, /device:TPU:0, one launch (start us, length us, event | category | flops | bytes accessed | tf_op | source)
XLA Modules:
  0.0 303.4 jit_solution(15027298163300527213)
XLA Ops:
  9.2 3.0 collective-permute-start
  12.1 3.1 %fusion.40 = f32[256]{0:T(256)S(1)} fusion(bf16[1,256,8192]{2,1,0:T(8,128)(2,1)} %param.13), kind=kLoop, calls=%fused_computation.47 | loop fusion | flops 6291200 | bytes 4195328 | tf_op jit(solution)/shard_map/reduce_sum | solution.py:96
  23.0 3.4 %convolution_convert_fusion.1 = bf16[256,8]{0,1:T(8,128)(2,1)S(1)} fusion(bf16[256,8192]{1,0:T(8,128)(2,1)} %copy-done.1, bf16[8,8192]{1,0:T(8,128)(2,1)S(1)} %copy-done), kind=kOutput, calls=%fused_computation.65 | convolution fusion | flops 33556480 | bytes 4329472 | tf_op jit(solution)/shard_map/dot_general | solution.py:67
  27.0 3.1 %fusion.44 = bf16[32,8,48,128]{3,1,2,0:T(8,128)(2,1)S(1)} fusion(bf16[256,8]{0,1:T(8,128)(2,1)S(1)} %convolution_convert_fusion.1, bf16[8,6144]{1,0:T(8,128)(2,1)} %param.20, bf16[1,256,6144]{2,1,0:T(8,128)(2,1)} %param.14), kind=kOutput, calls=%fused_computation.54 | convolution fusion | flops 31457280 | bytes 6393856 | tf_op jit(solution)/shard_map/dot_general | solution.py:103
  30.7 4.6 %copy.39 = bf16[1,256,6144]{1,2,0:T(8,128)(2,1)} copy(bf16[1,256,6144]{2,1,0:T(8,128)(2,1)} %param.17) | data formatting | bytes 6291456 | tf_op args[4]
  36.1 2.6 copy.65
  42.5 83.3 %while.12 = (s32[]{:T(128)}, bf16[6,256,8,128]{1,3,2,0:T(8,128)(2,1)}, f32[6,512,128]{1,2,0:T(8,128)}, bf16[6,512,128]{1,2,0:T(8,128)(2,1)}, pred[6,256,512]{1,2...) while((s32[]{:T(128)}, ...), condition=%wide.region_6.7_spmd, body=%wide.region_2.6_spmd.sunk | while | flops 1355807232 | bytes 50507916 | solution.py:56
  49.6 2.6 fusion.111
  52.2 4.3 %fusion.110 = bf16[6,256,8,128]{1,3,2,0:T(8,128)(2,1)} fusion(bf16[6,256,8,128]{1,3,2,0:T(8,128)(2,1)} %get-tuple-element.154, s32[]{:T(128)S(6)} %copy.73, f32[8,256]{1,0:T(8,128)S(1)} %bitcast.185, f32[8,256,512]{1,2,0:T(8,128)} %copy-done.3, f32[8,256]{1,0:T(8,128)S(1)} %get-tuple-element.143, bf16[6,512,128]{1,2,0:T(8,128)(2,1)} %get-tuple-element.165, ...), kind=kOutput, calls=%fused_computation.17.clone.1 | convolution fusion | flops 541327360 | bytes 6047744 | tf_op jit(solution)/shard_map/while/body/eval_jaxpr/gtu,ud->tgd/dot_general | solution.py:36
  63.5 2.6 fusion.111
  66.1 4.3 %fusion.110 = bf16[6,256,8,128]{1,3,2,0:T(8,128)(2,1)} fusion(bf16[6,256,8,128]{1,3,2,0:T(8,128)(2,1)} %get-tuple-element.154, s32[]{:T(128)S(6)} %copy.73, f32[8,256]{1,0:T(8,128)S(1)} %bitcast.185, f32[8,256,512]{1,2,0:T(8,128)} %copy-done.3, f32[8,256]{1,0:T(8,128)S(1)} %get-tuple-element.143, bf16[6,512,128]{1,2,0:T(8,128)(2,1)} %get-tuple-element.165, ...), kind=kOutput, calls=%fused_computation.17.clone.1 | convolution fusion | flops 541327360 | bytes 6047744 | tf_op jit(solution)/shard_map/while/body/eval_jaxpr/gtu,ud->tgd/dot_general | solution.py:36
  77.4 2.6 fusion.111
  80.0 4.2 %fusion.110 = bf16[6,256,8,128]{1,3,2,0:T(8,128)(2,1)} fusion(bf16[6,256,8,128]{1,3,2,0:T(8,128)(2,1)} %get-tuple-element.154, s32[]{:T(128)S(6)} %copy.73, f32[8,256]{1,0:T(8,128)S(1)} %bitcast.185, f32[8,256,512]{1,2,0:T(8,128)} %copy-done.3, f32[8,256]{1,0:T(8,128)S(1)} %get-tuple-element.143, bf16[6,512,128]{1,2,0:T(8,128)(2,1)} %get-tuple-element.165, ...), kind=kOutput, calls=%fused_computation.17.clone.1 | convolution fusion | flops 541327360 | bytes 6047744 | tf_op jit(solution)/shard_map/while/body/eval_jaxpr/gtu,ud->tgd/dot_general | solution.py:36
  91.3 2.6 fusion.111
  93.8 4.2 %fusion.110 = bf16[6,256,8,128]{1,3,2,0:T(8,128)(2,1)} fusion(bf16[6,256,8,128]{1,3,2,0:T(8,128)(2,1)} %get-tuple-element.154, s32[]{:T(128)S(6)} %copy.73, f32[8,256]{1,0:T(8,128)S(1)} %bitcast.185, f32[8,256,512]{1,2,0:T(8,128)} %copy-done.3, f32[8,256]{1,0:T(8,128)S(1)} %get-tuple-element.143, bf16[6,512,128]{1,2,0:T(8,128)(2,1)} %get-tuple-element.165, ...), kind=kOutput, calls=%fused_computation.17.clone.1 | convolution fusion | flops 541327360 | bytes 6047744 | tf_op jit(solution)/shard_map/while/body/eval_jaxpr/gtu,ud->tgd/dot_general | solution.py:36
  105.1 2.6 fusion.111
  107.7 4.2 %fusion.110 = bf16[6,256,8,128]{1,3,2,0:T(8,128)(2,1)} fusion(bf16[6,256,8,128]{1,3,2,0:T(8,128)(2,1)} %get-tuple-element.154, s32[]{:T(128)S(6)} %copy.73, f32[8,256]{1,0:T(8,128)S(1)} %bitcast.185, f32[8,256,512]{1,2,0:T(8,128)} %copy-done.3, f32[8,256]{1,0:T(8,128)S(1)} %get-tuple-element.143, bf16[6,512,128]{1,2,0:T(8,128)(2,1)} %get-tuple-element.165, ...), kind=kOutput, calls=%fused_computation.17.clone.1 | convolution fusion | flops 541327360 | bytes 6047744 | tf_op jit(solution)/shard_map/while/body/eval_jaxpr/gtu,ud->tgd/dot_general | solution.py:36
  121.5 4.3 %fusion.110 = bf16[6,256,8,128]{1,3,2,0:T(8,128)(2,1)} fusion(bf16[6,256,8,128]{1,3,2,0:T(8,128)(2,1)} %get-tuple-element.154, s32[]{:T(128)S(6)} %copy.73, f32[8,256]{1,0:T(8,128)S(1)} %bitcast.185, f32[8,256,512]{1,2,0:T(8,128)} %copy-done.3, f32[8,256]{1,0:T(8,128)S(1)} %get-tuple-element.143, bf16[6,512,128]{1,2,0:T(8,128)(2,1)} %get-tuple-element.165, ...), kind=kOutput, calls=%fused_computation.17.clone.1 | convolution fusion | flops 541327360 | bytes 6047744 | tf_op jit(solution)/shard_map/while/body/eval_jaxpr/gtu,ud->tgd/dot_general | solution.py:36
  128.4 3.6 %convolution_multiply_fusion.1 = f32[8,6144]{1,0:T(8,128)} fusion(bf16[256,8]{0,1:T(8,128)(2,1)S(1)} %copy-done.11, bf16[256,6144]{0,1:T(8,128)(2,1)} %bitcast.178), kind=kOutput, calls=%fused_computation.51 | convolution fusion | flops 25214976 | bytes 3346432 | tf_op jit(solution)/shard_map/dot_general | solution.py:61
  135.1 4.5 %fusion.55 = f32[256,8192]{1,0:T(8,128)} fusion(bf16[256,8]{0,1:T(8,128)(2,1)S(1)} %fusion.47, bf16[8,8192]{1,0:T(8,128)(2,1)S(1)} %copy-done), kind=kOutput, calls=%fused_computation.94 | convolution fusion | flops 33554432 | bytes 8523776 | tf_op jit(solution)/shard_map/dot_general | solution.py:144
  139.6 4.4 %collective-permute-done.2 = bf16[256,6,128]{0,2,1:T(8,128)(2,1)S(1)} collective-permute-done((bf16[256,6,128]{0,2,1:T(8,128)(2,1)S(1)}, bf16[256,6,128]{0,2,1:T(8,128)(2,1)S(1)}, u32[]{:S(2)}, u32[]{:S(2)}) %collective-permute-start.2) | collective-permute-done | bytes 393248 | tf_op jit(solution)/shard_map/ppermute | solution.py:18
  145.7 6.4 %fusion.43 = f32[8192]{0:T(1024)S(1)} fusion(f32[256]{0:T(256)S(1)} %copy-done.15, bf16[1,256,8192]{2,1,0:T(8,128)(2,1)} %param.13, f32[256,8192]{1,0:T(8,128)} %fusion.55, bf16[256,8]{0,1:T(8,128)(2,1)S(1)} %fusion.48, bf16[8,8192]{1,0:T(8,128)(2,1)S(1)} %copy-done.6), kind=kOutput, calls=%fused_computation.53 | convolution fusion | flops 44032000 | bytes 12751872 | tf_op jit(solution)/shard_map/dot_general | solution.py:146
  152.4 41.0 %all-reduce = (f32[8,768]{1,0:T(8,128)S(1)}, f32[8192]{0:T(1024)S(1)}) all-reduce(f32[8,768]{1,0:T(8,128)S(1)} %convolution_multiply_fusion.3, f32[8192]{0:T(1024)S(1)} %fusion.43), channel_id=1, replica_groups=mesh['seq'=4,'dp'=8] {'seq','dp'}, use_global_device_ids=true, to_apply=%region_13.14 | all-reduce | flops 14336 | bytes 114688 | tf_op jit(solution)/shard_map/psum | solution.py:159
  194.7 89.1 %all-reduce.4.cloned.1.call-done = (f32[8,8192]{1,0:T(8,128)}, f32[8,6144]{1,0:T(8,128)}, f32[8,8192]{1,0:T(8,128)}) async-done(((f32[8,8192]{1,0:T(8,128)}, f32[8,6144]{1,0:T(8,128)}, f32[8,8192]{1,0:T(8,128)}), (f32[8,8192]{1,0:T(8,128)}, f32[8,6144]{1,0:T(8,128)}, f32[8,8192]{1,0:T(8,128)})) %all-reduce.4.cloned.1.call-update) | async-done | bytes 720912 | tf_op jit(solution)/shard_map/psum | solution.py:159
  (131 shorter events, 78.5 us)
Async XLA Ops:
  7.2 15.8 %copy-start = (bf16[8,8192]{1,0:T(8,128)(2,1)S(1)}, bf16[8,8192]{1,0:T(8,128)(2,1)}, u32[]{:S(2)}) copy-start(bf16[8,8192]{1,0:T(8,128)(2,1)} %param.19) | copy-start | bytes 393220
  7.2 8.1 %copy-start.13 = (bf16[8192]{0:T(1024)(128)(2,1)S(1)}, bf16[8192]{0:T(1024)(128)(2,1)}, u32[]{:S(2)}) copy-start(bf16[8192]{0:T(1024)(128)(2,1)} %param.18) | copy-start | bytes 49156
  7.2 276.6 %all-reduce.4.cloned.1.call-start = ((), (), s32[]{:S(2)}) async-start(), calls=%async_computation | async-start | bytes 1441792 | tf_op jit(solution)/shard_map/psum | solution.py:159
  9.2 6.1 %copy-start.4 = (bf16[1,256,8192]{2,1,0:T(8,128)(2,1)S(1)}, bf16[1,256,8192]{2,1,0:T(8,128)(2,1)}, u32[]{:S(2)}) copy-start(bf16[1,256,8192]{2,1,0:T(8,128)(2,1)} %param.13) | copy-start | bytes 12582916
  9.2 30.1 %collective-permute-start = (bf16[256,6,128]{0,2,1:T(8,128)(2,1)}, bf16[256,6,128]{0,2,1:T(8,128)(2,1)}, u32[]{:S(2)}, u32[]{:S(2)}) collective-permute-start(bf16[256,6,128]{0,2,1:T(8,128)(2,1)} %bitcast.17), channel_id=1, source_target_pairs={{24,0},{0,8},{8,16},{16,24},{25,1},{1,9},{9,17},{17,25},{26,2},{2,... | collective-permute-start | bytes 1179656 | tf_op jit(solution)/shard_map/ppermute | solution.py:18
  15.2 1.2 copy-start.14
  15.3 3.1 %copy-start.6 = (bf16[8,8192]{1,0:T(8,128)(2,1)S(1)}, bf16[8,8192]{1,0:T(8,128)(2,1)}, u32[]{:S(2)}) copy-start(bf16[8,8192]{1,0:T(8,128)(2,1)} %param.21) | copy-start | bytes 393220
  16.5 1.9 copy-start.1
  18.4 4.5 %copy-start.17 = (s32[6]{0:T(128)S(1)}, s32[6]{0:T(128)}, u32[]{:S(2)}) copy-start(s32[6]{0:T(128)} %param.23) | copy-start | bytes 76
  20.9 20.5 %collective-permute-start.1 = (bf16[256,6,128]{0,2,1:T(8,128)(2,1)}, bf16[256,6,128]{0,2,1:T(8,128)(2,1)}, u32[]{:S(2)}, u32[]{:S(2)}) collective-permute-start(bf16[256,6,128]{0,2,1:T(8,128)(2,1)} %bitcast.24), channel_id=1, source_target_pairs={{24,0},{0,8},{8,16},{16,24},{25,1},{1,9},{9,17},{17,25},{26,2},{2,... | collective-permute-start | bytes 1179656 | tf_op jit(solution)/shard_map/ppermute | solution.py:18
  26.4 3.7 %copy-start.16 = (pred[512]{0:T(512)(128)(4,1)S(1)}, pred[512]{0:T(512)(128)(4,1)}, u32[]{:S(2)}) copy-start(pred[512]{0:T(512)(128)(4,1)} %iota_compare_fusion.2) | copy-start | bytes 1540
  36.1 2.6 copy-start.12
  42.5 83.3 %copy-start.7 = (bf16[8,6144]{1,0:T(8,128)(2,1)S(1)}, bf16[8,6144]{1,0:T(8,128)(2,1)}, u32[]{:S(2)}) copy-start(bf16[8,6144]{1,0:T(8,128)(2,1)} %param.20) | copy-start | bytes 294916
  42.5 85.8 %copy-start.11 = (bf16[256,8]{0,1:T(8,128)(2,1)S(1)}, bf16[256,8]{0,1:T(8,128)(2,1)}, u32[]{:S(2)}) copy-start(bf16[256,8]{0,1:T(8,128)(2,1)} %copy-done.10) | copy-start | bytes 12292
  47.7 2.0 copy-start.3
  61.5 2.0 copy-start.3
  75.4 2.0 copy-start.3
  89.3 2.0 copy-start.3
  103.2 2.0 copy-start.3
  117.0 2.0 copy-start.3
  125.8 6.2 %copy-start.2 = (bf16[256,8192]{1,0:T(8,128)(2,1)S(1)}, bf16[256,8192]{1,0:T(8,128)(2,1)}, u32[]{:S(2)}) copy-start(bf16[256,8192]{1,0:T(8,128)(2,1)} %copy-done.1) | copy-start | bytes 12582916
  128.4 5.0 %copy-start.5 = (f32[6,512,128]{1,2,0:T(8,128)S(1)}, f32[6,512,128]{1,2,0:T(8,128)}, u32[]{:S(2)}) copy-start(f32[6,512,128]{1,2,0:T(8,128)} %get-tuple-element.49) | copy-start | bytes 4718596
  133.4 10.6 %collective-permute-start.2 = (bf16[256,6,128]{0,2,1:T(8,128)(2,1)S(1)}, bf16[256,6,128]{0,2,1:T(8,128)(2,1)S(1)}, u32[]{:S(2)}, u32[]{:S(2)}) collective-permute-start(bf16[256,6,128]{0,2,1:T(8,128)(2,1)S(1)} %slice.19), channel_id=1, source_target_pairs={{8,0},{16,8},{24,16},{0,24},{9,1},{17,9},{25,17},{1,25},{10,2},{18... | collective-permute-start | bytes 1179656 | tf_op jit(solution)/shard_map/ppermute | solution.py:18
  139.6 6.1 %copy-start.15 = (f32[256]{0:T(256)S(1)}, f32[256]{0:T(256)}, u32[]{:S(2)}) copy-start(f32[256]{0:T(256)} %copy-done.14) | copy-start | bytes 3076
  (3 other events, 3.0 us)
Sparse Core Ops, SparseCore 0:
  152.3 131.4 all-reduce.3
where the time goes:
time: 305 us; the launch traced here: 303 us
  waiting for transfers between devices  93.6 us (31%)
  matrix products  86.9 us (28%)
  blocking collectives  41 us (13%)
  other arithmetic  33.8 us (11%)
  local copies, waits for them, and re-layouts  24.2 us (8%)
  between operations  17.5 us (6%)
  starting transfers between devices  6.21 us (2%)
    psum x1, waiting for transfers between devices, shards(): lax.psum((raw_qa, query_up_unscaled, raw_va, value_up_unscaled, raw_gain)...  89.1 us
    psum x1, blocking collectives, shards(): lax.psum((raw_qa, query_up_unscaled, raw_va, value_up_unscaled, raw_gain)...  41 us
    dot_general x6, matrix products, attend(): jnp.einsum('gtu,ud->tgd', dscore, key_rows, preferred_element_type=jnp.fl...  25.5 us
    dot_general x6, matrix products, attend(): jnp.einsum('gtu,tgd->ud', weights, grad_out, preferred_element_type=jnp.f...  15.4 us
    dot_general x6, matrix products, attend(): jnp.einsum('tgd,ud->gtu', query_rows, key_rows, preferred_element_type=jn...  11.1 us
    sub x6, other arithmetic, attend(): exponent = jnp.exp(scores - row_max)  11.1 us
    unnamed x37, local copies, waits for them, and re-layouts  9.64 us
    dynamic_slice x12, local copies, waits for them, and re-layouts, all_heads(): query_gradient, value_gradient = lax.map(attend_heads, operands)  8.13 us
  transfers between devices with their start and end apart: 4, of which 2 were waited for; matrix products, arithmetic and copies ran while one was open for 10% of the time, Pallas kernels for 0%

commit v1 on v0

v1 whole, which is shorter than its diff:
```python
import functools
import math

import jax
import jax.numpy as jnp
from jax import lax
from jax.experimental import pallas as pl
from jax.experimental.pallas import tpu as pltpu
from jax.sharding import PartitionSpec as P

HEAD_SIZE = 128
CORES = 2
LANES = 128


EPS = 1e-05
ADAPTER_SCALE = 2.0
F32 = jnp.float32
BF16 = jnp.bfloat16
NT = (((1,), (1,)), ((), ()))
NN = (((1,), (0,)), ((), ()))


def from_behind(block, axis, distance):
    devices = range(lax.axis_size(axis))
    route = [((i - distance) % len(devices), i) for i in devices]
    return lax.ppermute(block, axis, route)


def dot(left, right, dims):
    return lax.dot_general(left, right, dims, preferred_element_type=F32)


def prologue_kernel(x_ref, scale_ref, down_ref, fv_ref, vup_ref, inv_ref, mid_ref, value_ref):
    width = x_ref.shape[1]
    rank = vup_ref.shape[0]
    hidden = x_ref[...].astype(F32)
    inverse = lax.rsqrt(jnp.sum(hidden * hidden, axis=-1, keepdims=True) * (1.0 / width) + EPS)
    inv_ref[...] = inverse
    normed = (hidden * inverse * scale_ref[...].astype(F32)).astype(BF16)
    mid = dot(normed, down_ref[...], NT).astype(BF16)
    mid_ref[...] = mid
    value_mid = mid[:, rank:] * ADAPTER_SCALE
    value_ref[...] = (
        fv_ref[...].astype(F32) + dot(value_mid.astype(BF16), vup_ref[...], NN)
    ).astype(BF16)


def prologue(x, scale, down, frozen_values, vup, steps):
    rows, width = x.shape
    block = rows // steps
    kv = frozen_values.shape[1]
    ranks = down.shape[0]
    whole = lambda i: (0, 0)
    by_rows = lambda i: (i, 0)
    return pl.pallas_call(
        prologue_kernel,
        grid=(steps,),
        in_specs=[
            pl.BlockSpec((block, width), by_rows),
            pl.BlockSpec((1, width), whole),
            pl.BlockSpec((ranks, width), whole),
            pl.BlockSpec((block, kv), by_rows),
            pl.BlockSpec(vup.shape, whole),
        ],
        out_specs=[
            pl.BlockSpec((block, 1), by_rows),
            pl.BlockSpec((block, ranks), by_rows),
            pl.BlockSpec((block, kv), by_rows),
        ],
        out_shape=[
            jax.ShapeDtypeStruct((rows, 1), F32),
            jax.ShapeDtypeStruct((rows, ranks), BF16),
            jax.ShapeDtypeStruct((rows, kv), BF16),
        ],
        cost_estimate=pl.CostEstimate(
            flops=40 * rows * width, bytes_accessed=2 * rows * width, transcendentals=0
        ),
        name="prologue",
    )(x, scale, down, frozen_values, vup)


def attention_kernel(
    order_ref,
    fq_ref,
    grad_ref,
    key_ref,
    prior_key_ref,
    value_ref,
    prior_value_ref,
    mid_ref,
    mid_t_ref,
    up_ref,
    dv_ref,
    dv_prior_ref,
    qb_ref,
    dq_mid_ref,
):
    head = pl.program_id(0)
    rows = fq_ref.shape[0]
    heads = fq_ref.shape[1] // HEAD_SIZE
    rank = up_ref.shape[0]
    factor = 1.0 / math.sqrt(HEAD_SIZE)
    displaced = order_ref[0] == head
    for i in range(1, order_ref.shape[0] // 2):
        displaced = jnp.logical_or(displaced, order_ref[i] == head)
    odd = lax.rem(lax.axis_index("seq"), 2) == 1
    needs_prior = jnp.logical_xor(displaced, odd)

    @pl.when(head == 0)
    def _():
        dq_mid_ref[...] = jnp.zeros_like(dq_mid_ref)

    def run(with_prior):
        keys = key_ref[...]
        values = value_ref[...]
        if with_prior:
            keys = jnp.concatenate([keys, prior_key_ref[...]], axis=0)
            values = jnp.concatenate([values, prior_value_ref[...]], axis=0)
        keys_t = keys.T
        query_mid = mid_ref[:, :rank] * ADAPTER_SCALE
        mid_t = (mid_t_ref[:rank] * ADAPTER_SCALE).astype(BF16)
        key_pos = lax.broadcasted_iota(jnp.int32, (rows, rows), 0)
        query_pos = lax.broadcasted_iota(jnp.int32, (rows, rows), 1)
        causal = key_pos <= query_pos
        dv = None
        dq_mid = dq_mid_ref[...]
        for j in range(heads):
            cols = slice(j * HEAD_SIZE, (j + 1) * HEAD_SIZE)
            up = up_ref[:, cols]
            query = (
                fq_ref[:, cols].astype(F32) + dot(query_mid.astype(BF16), up, NN)
            ).astype(BF16)
            grad = grad_ref[:, cols]
            scores = dot(keys, query, NT)
            own = jnp.where(causal, scores[:rows], -jnp.inf)
            if with_prior:
                scores = jnp.concatenate([own, scores[rows:]], axis=0)
            else:
                scores = own
            top = jnp.max(scores, axis=0, keepdims=True)
            exponent = jnp.exp2((scores - top) * (factor * math.log2(math.e)))
            probs = exponent * (1.0 / jnp.sum(exponent, axis=0, keepdims=True))
            weights = probs.astype(BF16)
            dprob = dot(values, grad, NT)
            delta = jnp.sum(weights.astype(F32) * dprob, axis=0, keepdims=True)
            dscore = (probs * (dprob - delta)).astype(BF16)
            term = dot(weights, grad, NN)
            dv = term if dv is None else dv + term
            dquery = (dot(keys_t, dscore, NN) * factor).astype(BF16)
            qb_ref[:, cols] = dot(mid_t, dquery, NT)
            dq_mid = dq_mid + dot(up, dquery, NN)
        dq_mid_ref[...] = dq_mid
        dv_ref[...] = dv[:rows]
        if with_prior:
            dv_prior_ref[...] = dv[rows:].astype(BF16)
        else:
            dv_prior_ref[...] = jnp.zeros_like(dv_prior_ref)

    @pl.when(needs_prior)
    def _():
        run(True)

    @pl.when(jnp.logical_not(needs_prior))
    def _():
        run(False)


def attention(order, fq, grads, keys, prior_keys, values, prior_values, mid, mid_t, up):
    rows, queries = fq.shape
    kv = keys.shape[1]
    kv_heads = kv // HEAD_SIZE
    wide = queries // kv_heads
    rank = up.shape[0]
    by_head = lambda h, order: (0, h)
    whole = lambda h, order: (0, 0)
    narrow = pl.BlockSpec((rows, HEAD_SIZE), by_head)
    broad = pl.BlockSpec((rows, wide), by_head)
    return pl.pallas_call(
        attention_kernel,
        grid_spec=pltpu.PrefetchScalarGridSpec(
            num_scalar_prefetch=1,
            grid=(kv_heads,),
            in_specs=[
                broad,
                broad,
                narrow,
                narrow,
                narrow,
                narrow,
                pl.BlockSpec(mid.shape, whole),
                pl.BlockSpec(mid_t.shape, whole),
                pl.BlockSpec((rank, wide), by_head),
            ],
            out_specs=[
                narrow,
                narrow,
                pl.BlockSpec((rank, wide), by_head),
                pl.BlockSpec((rank, rows), whole),
            ],
        ),
        out_shape=[
            jax.ShapeDtypeStruct((rows, kv), F32),
            jax.ShapeDtypeStruct((rows, kv), BF16),
            jax.ShapeDtypeStruct((rank, queries), F32),
            jax.ShapeDtypeStruct((rank, rows), F32),
        ],
        cost_estimate=pl.CostEstimate(
            flops=12 * rows * rows * queries,
            bytes_accessed=4 * rows * queries,
            transcendentals=0,
        ),
        name="attention",
    )(order, fq, grads, keys, prior_keys, values, prior_values, mid, mid_t, up)


def epilogue_kernel(
    x_ref,
    inv_ref,
    scale_ref,
    down_ref,
    dq_mid_ref,
    dv_ref,
    handed_ref,
    vup_ref,
    mid_t_ref,
    qb_ref,
    packed_ref,
    inner_ref,
    gain_ref,
):
    step = pl.program_id(0)
    block = x_ref.shape[1]
    rank = vup_ref.shape[0]
    width = block * pl.num_programs(0)
    full = gain_ref.shape[0] * block
    queries = qb_ref.shape[1]
    kv = dv_ref.shape[1]

    @pl.when(step == 0)
    def _():
        dv = (dv_ref[...] + handed_ref[...].astype(F32)).astype(BF16)
        mid_t = (mid_t_ref[rank:] * ADAPTER_SCALE).astype(BF16)
        packed_ref[:, 2 * full : 2 * full + queries] = qb_ref[...].astype(BF16)
        packed_ref[:, 2 * full + queries : 2 * full + queries + kv] = dot(mid_t, dv, NN).astype(
            BF16
        )
        dv_mid = dot(vup_ref[...], dv, NT)
        inner_ref[...] = (
            ADAPTER_SCALE * jnp.concatenate([dq_mid_ref[...], dv_mid], axis=0)
        ).astype(BF16)
        gain_ref[...] = jnp.zeros_like(gain_ref)
        used = 2 * full + queries + kv + block
        if used < packed_ref.shape[1]:
            packed_ref[:, used:] = jnp.zeros((rank, packed_ref.shape[1] - used), BF16)

    inner = inner_ref[...]
    unit = x_ref[...].astype(F32) * inv_ref[...]
    normed = (unit * scale_ref[...].astype(F32)).astype(BF16)
    raw = dot(inner, normed, NN).astype(BF16)
    at = pl.multiple_of(step * block, block)
    packed_ref[:, pl.ds(at, block)] = raw[:rank]
    packed_ref[:, pl.ds(at + full, block)] = raw[rank:]
    gain = jnp.sum(
        down_ref[...].astype(F32) * dot(inner, unit.astype(BF16), NN), axis=0, keepdims=True
    )
    row = lax.broadcasted_iota(jnp.int32, gain_ref.shape, 0)
    gain_ref[...] = jnp.where(row == step, gain, gain_ref[...])

    @pl.when(step == pl.num_programs(0) - 1)
    def _():
        base = 2 * full + queries + kv
        packed_ref[:, base : base + block] = gain_ref[...].astype(BF16)


def epilogue(x, inverse, scale, down, dq_mid, dv, handed, vup, mid_t, qb, total):
    rows, width = x.shape
    rank = vup.shape[0]
    block = width // rank
    whole = lambda j: (0, 0)
    by_cols = lambda j: (0, j)
    kept = lambda a: pl.BlockSpec(a.shape, whole)
    return pl.pallas_call(
        epilogue_kernel,
        grid=(rank,),
        in_specs=[
            pl.BlockSpec((rows, block), by_cols),
            kept(inverse),
            pl.BlockSpec((1, block), by_cols),
            pl.BlockSpec((down.shape[0], block), by_cols),
            kept(dq_mid),
            kept(dv),
            kept(handed),
            kept(vup),
            kept(mid_t),
            kept(qb),
        ],
        out_specs=pl.BlockSpec((rank, total), whole),
        out_shape=jax.ShapeDtypeStruct((rank, total), BF16),
        scratch_shapes=[
            pltpu.VMEM((2 * rank, rows), BF16),
            pltpu.VMEM((rank, block), F32),
        ],
        cost_estimate=pl.CostEstimate(
            flops=80 * rows * width, bytes_accessed=2 * rows * width, transcendentals=0
        ),
        name="epilogue",
    )(x, inverse, scale, down, dq_mid, dv, handed, vup, mid_t, qb)


def reduce_kernel(
    seqs,
    planes,
    limit,
    packed_ref,
    qa_ref,
    qb_ref,
    va_ref,
    vb_ref,
    gain_ref,
    parts,
    column,
    full,
    send_one,
    recv_one,
    send_two,
    recv_two,
    send_three,
    recv_three,
):
    group = seqs * CORES
    piece = full.shape[1] // group
    place = lax.axis_index("dp")
    plane = place // CORES
    me = lax.axis_index("seq") * CORES + place % CORES

    def in_group(k):
        peer = lax.rem(me + k, group)
        return peer, {"seq": peer // CORES, "dp": plane * CORES + peer % CORES}

    def in_column(k):
        return {"dp": lax.rem(plane + k, planes) * CORES + place % CORES}

    def span(index):
        return pl.ds(pl.multiple_of(index * piece, piece), piece)

    barrier = pltpu.get_barrier_semaphore()
    for k in range(1, group):
        pl.semaphore_signal(
            barrier, inc=1, device_id=in_group(k)[1], device_id_type=pl.DeviceIdType.MESH
        )
    for k in range(1, planes):
        pl.semaphore_signal(
            barrier, inc=1, device_id=in_column(k), device_id_type=pl.DeviceIdType.MESH
        )
    pl.semaphore_wait(barrier, group + planes - 2)

    def remote(source, target, send, recv, device):
        copy = pltpu.make_async_remote_copy(
            src_ref=source,
            dst_ref=target,
            send_sem=send,
            recv_sem=recv,
            device_id=device,
            device_id_type=pl.DeviceIdType.MESH,
        )
        copy.start()
        return copy

    first = []
    for k in range(1, group):
        peer, device = in_group(k)
        first.append(
            remote(
                packed_ref.at[:, span(peer)],
                parts.at[k - 1],
                send_one.at[k - 1],
                recv_one.at[k - 1],
                device,
            )
        )
    total = packed_ref[:, span(me)].astype(F32)
    for k in range(1, group):
        first[k - 1].wait_recv()
        total = total + parts[k - 1].astype(F32)
    column[plane] = total.astype(BF16)
    second = [
        remote(
            column.at[plane],
            column.at[plane],
            send_two.at[k - 1],
            recv_two.at[k - 1],
            in_column(k),
        )
        for k in range(1, planes)
    ]
    for copy in second:
        copy.wait_recv()
    total = column[0].astype(F32)
    for i in range(1, planes):
        total = total + column[i].astype(F32)
    full[:, span(me)] = total.astype(BF16)
    third = [
        remote(
            full.at[:, span(me)],
            full.at[:, span(me)],
            send_three.at[k - 1],
            recv_three.at[k - 1],
            in_group(k)[1],
        )
        for k in range(1, group)
    ]
    for copy in third:
        copy.wait_recv()
    for copy in first + second + third:
        copy.wait_send()
    sums = full[...].astype(F32)
    squares = jnp.sum(jnp.sum(sums * sums, axis=1, keepdims=True), axis=0, keepdims=True)
    scale = jnp.minimum(1.0, limit / jnp.sqrt(squares))
    at = 0
    for out in (qa_ref, va_ref, qb_ref, vb_ref, gain_ref):
        out[...] = full[:, at : at + out.shape[1]].astype(F32) * scale
        at += out.shape[1]


def reduced(packed, seqs, planes, limit, widths):
    rank, total = packed.shape
    group = seqs * CORES
    piece = total // group
    vmem = pl.BlockSpec(memory_space=pltpu.VMEM)
    dma = pltpu.SemaphoreType.DMA
    return pl.pallas_call(
        functools.partial(reduce_kernel, seqs, planes, limit),
        in_specs=[vmem],
        out_specs=[vmem] * len(widths),
        out_shape=[jax.ShapeDtypeStruct((rank, w), F32) for w in widths],
        scratch_shapes=[
            pltpu.VMEM((group - 1, rank, piece), BF16),
            pltpu.VMEM((planes, rank, piece), BF16),
            pltpu.VMEM((rank, total), BF16),
            dma((group - 1,)),
            dma((group - 1,)),
            dma((max(planes - 1, 1),)),
            dma((max(planes - 1, 1),)),
            dma((group - 1,)),
            dma((group - 1,)),
        ],
        compiler_params=pltpu.CompilerParams(collective_id=0, has_side_effects=True),
        name="reduced",
    )(packed)


def shards(
    layer_input,
    frozen_queries,
    frozen_keys,
    frozen_values,
    output_gradient,
    norm_scale_vector,
    query_down_weight,
    query_up_weight,
    value_down_weight,
    value_up_weight,
    head_ordering,
):
    seqs = lax.axis_size("seq")
    planes = lax.axis_size("dp") // CORES
    rank, width = query_down_weight.shape
    queries = query_up_weight.shape[1]
    kv = value_up_weight.shape[1]
    scale = norm_scale_vector.reshape(1, width)
    down = jnp.concatenate([query_down_weight, value_down_weight], axis=0)
    keys = frozen_keys[0]
    prior_keys = from_behind(keys, "seq", 1)
    inverse, mid, values = prologue(
        layer_input[0], scale, down, frozen_values[0], value_up_weight, 4
    )
    mid_t = mid.T
    prior_values = from_behind(values, "seq", 1)
    dv, dv_prior, qb, dq_mid = attention(
        head_ordering,
        frozen_queries[0],
        output_gradient[0],
        keys,
        prior_keys,
        values,
        prior_values,
        mid,
        mid_t,
        query_up_weight,
    )
    handed = from_behind(dv_prior, "seq", -1)
    used = 2 * width + queries + kv + width // rank
    unit = seqs * CORES * LANES
    total = -(-used // unit) * unit
    packed = epilogue(
        layer_input[0], inverse, scale, down, dq_mid, dv, handed, value_up_weight, mid_t, qb, total
    )
    limit = math.sqrt(rank * (2 * width + queries + kv) + width)
    qa, gqb, va, vb, gain = reduced(
        packed, seqs, planes, limit, (width, queries, width, kv, width // rank)
    )
    return (qa, gqb, va, vb, gain.reshape(width))


def solution(mesh):
    placed = (
        P("dp", "seq", None),
        P("dp", "seq", None),
        P("dp", "seq", None),
        P("dp", "seq", None),
        P("dp", "seq", None),
        P(),
        P(),
        P(),
        P(),
        P(),
        P(),
    )
    return jax.shard_map(
        shards, mesh=mesh, in_specs=placed, out_specs=(P(), P(), P(), P(), P()), check_vma=False
    )
```

time: 305 us -> 117 us (0.38)
  matrix products: 86.9 us -> 0 us
  Pallas kernels: 0 us -> 77.3 us
  waiting for transfers between devices: 93.6 us -> 18.3 us
  blocking collectives: 41 us -> 0 us
  other arithmetic: 33.8 us -> 0 us
  between operations: 17.5 us -> 0.67 us
  local copies, waits for them, and re-layouts: 24.2 us -> 14.6 us
    psum x1 -> x0, waiting for transfers between devices: 89.1 us -> none  [shards(): lax.psum((raw_qa, query_up_unscaled, raw_va, value_up_unscaled, raw_gain)...]
    dot_general x36 -> x0, matrix products: 86.9 us -> none  [the longest x6 25.5 us: attend(): jnp.einsum('gtu,ud->tgd', dscore, key_rows, preferred_element_type=jnp.fl...]
    pallas_call x0 -> x4, Pallas kernels: none -> 77.3 us  [the longest x1 41 us: attention(): pl.pallas_call(attention_kernel, grid_spec=pltpu.PrefetchScalarGridSpec(n...]
    psum x1 -> x0, blocking collectives: 41 us -> none  [shards(): lax.psum((raw_qa, query_up_unscaled, raw_va, value_up_unscaled, raw_gain)...]
    ppermute x3, waiting for transfers between devices: 4.4 us -> 18.3 us  [from_behind(): return lax.ppermute(block, axis, route)]
    sub x7 -> x0, other arithmetic: 11.1 us -> none  [the longest x6 11.1 us: attend(): exponent = jnp.exp(scores - row_max)]
    reduce_sum x6 -> x0, other arithmetic: 9.18 us -> none  [the longest x5 6.07 us: squares_of(): total = total + jnp.sum(part * part)]
    dynamic_slice x12 -> x0, local copies, waits for them, and re-layouts: 8.13 us -> none  [all_heads(): query_gradient, value_gradient = lax.map(attend_heads, operands)]
  transfers between devices with their start and end apart: 4 -> 3, of which waited for: 2 -> 2; matrix products, arithmetic and copies ran while one was open for 10% -> 4% of each run, Pallas kernels for 0% -> 5%
where the time goes in v1:
time: 117 us; the launch traced here: 116 us
  Pallas kernels  77.3 us (66%)
  waiting for transfers between devices  18.3 us (16%)
  local copies, waits for them, and re-layouts  14.6 us (12%)
  starting transfers between devices  4.93 us (4%)
    pallas_call x1, Pallas kernels, attention(): pl.pallas_call(attention_kernel, grid_spec=pltpu.PrefetchScalarGridSpec(n...  41 us
    pallas_call x1, Pallas kernels, reduced(): pl.pallas_call(functools.partial(reduce_kernel, seqs, planes, limit), in_...  22.1 us
    ppermute x3, waiting for transfers between devices, from_behind(): return lax.ppermute(block, axis, route)  18.3 us
    unnamed x14, local copies, waits for them, and re-layouts  10.8 us
    pallas_call x1, Pallas kernels, epilogue(): pl.pallas_call(epilogue_kernel, grid=(rank,), in_specs=[pl.BlockSpec((row...  7.98 us
    pallas_call x1, Pallas kernels, prologue(): pl.pallas_call(prologue_kernel, grid=(steps,), in_specs=[pl.BlockSpec((bl...  6.23 us
    ppermute x3, starting transfers between devices, from_behind(): return lax.ppermute(block, axis, route)  4.93 us
  transfers between devices with their start and end apart: 3, of which 2 were waited for; matrix products, arithmetic and copies ran while one was open for 4% of the time, Pallas kernels for 5%

profile of v1, /device:TPU:0, one launch (start us, length us, event | category | flops | bytes accessed | tf_op | source)
XLA Modules:
  0.0 115.7 jit_solution(1294530705567856870)
XLA Ops:
  0.6 3.0 %collective-permute-start = (bf16[256,768]{1,0:T(8,128)(2,1)}, bf16[256,768]{1,0:T(8,128)(2,1)S(1)}, u32[]{:S(2)}, u32[]{:S(2)}) collective-permute-start(bf16[256,768]{1,0:T(8,128)(2,1)} %bitcast.19), channel_id=1, source_target_pairs={{24,0},{0,8},{8,16},{16,24},{25,1},{1,9},{9,17},{17,25},{26,2},{2,... | collective-permute-start | bytes 1179656 | tf_op jit(solution)/shard_map/ppermute | solution.py:27
  3.6 1.3 %reshape.16.scale_ref = bf16[1,8192]{1,0:T(2,128)(2,1)} reshape(bf16[8192]{0:T(1024)(128)(2,1)} %param.16) | data formatting | bytes 32768 | tf_op jit(solution)/shard_map/reshape | solution.py:471
  5.0 0.9 constant_dynamic-update-slice_fusion.1
  5.9 0.9 constant_dynamic-update-slice_fusion.down_ref
  6.8 0.0 copy-start
  6.8 0.7 copy-done
  7.5 6.2 %prologue.1 = (f32[256,1]{1,0:T(8,128)}, bf16[256,16]{1,0:T(8,128)(2,1)}, bf16[256,768]{1,0:T(8,128)(2,1)}) custom-call(bf16[256,8192]{1,0:T(8,128)(2,1)} %bitcast.10, bf16[1,8192]{1,0:T(2,128)(2,1)} %reshape.16.scale_ref, bf16[16,8192]{1,0:T(8,128)(2,1)} %copy-done, bf16[256,768]{1,0:T(8,128)(2,1)} %bitcast.12, bf16[8,768]{1,0:T(8,128)(2,1)} %vup_ref.3), custom_call_target="tpu_custom_call" | custom-call | flops 83886080 | bytes 4194304 | tf_op jit(solution)/shard_map/prologue/pallas_call | solution.py:56
  13.8 1.5 %collective-permute-start.1 = (bf16[256,768]{1,0:T(8,128)(2,1)}, bf16[256,768]{1,0:T(8,128)(2,1)S(1)}, u32[]{:S(2)}, u32[]{:S(2)}) collective-permute-start(bf16[256,768]{1,0:T(8,128)(2,1)} %get-tuple-element.18.value_ref), channel_id=1, source_target_pairs={{24,0},{0,8},{8,16},{16,24},{25,1},{1,9},{9,17},{17,25},{26,2},{2,... | collective-permute-start | bytes 1179656 | tf_op jit(solution)/shard_map/ppermute | solution.py:27
  15.3 1.5 %copy.16 = bf16[256,16]{0,1:T(8,128)(2,1)} copy(bf16[256,16]{1,0:T(8,128)(2,1)} %get-tuple-element.19.mid_ref) | data formatting | bytes 16384 | tf_op jit(solution)/shard_map/prologue/pallas_call | solution.py:56
  16.8 0.0 collective-permute-done.prior_key_ref
  16.8 8.7 %collective-permute-done.1.prior_value_ref = bf16[256,768]{1,0:T(8,128)(2,1)S(1)} collective-permute-done((bf16[256,768]{1,0:T(8,128)(2,1)}, bf16[256,768]{1,0:T(8,128)(2,1)S(1)}, u32[]{:S(2)}, u32[]{:S(2)}) %collective-permute-start.1) | collective-permute-done | bytes 393248 | tf_op jit(solution)/shard_map/ppermute | solution.py:27
  25.5 0.0 copy-done.2
  25.5 0.7 copy-done.3
  26.2 41.0 %attention.1 = (f32[256,768]{1,0:T(8,128)}, bf16[256,768]{1,0:T(8,128)(2,1)}, f32[8,6144]{1,0:T(8,128)}, f32[8,256]{1,0:T(8,128)}) custom-call(s32[6]{0:T(128)} %order_ref.1, bf16[256,6144]{1,0:T(8,128)(2,1)} %bitcast.17, bf16[256,6144]{1,0:T(8,128)(2,1)} %bitcast.18, bf16[256,768]{1,0:T(8,128)(2,1)} %bitcast.20, bf16[256,768]{1,0:T(8,128)(2,1)} %copy-done.2, ...), custom_call_target="tpu_custom_call" | custom-call | flops 4831838208 | bytes 6291456 | tf_op jit(solution)/shard_map/attention/pallas_call | solution.py:179
  67.2 0.4 collective-permute-start.2
  67.6 9.6 %collective-permute-done.2.handed_ref = bf16[256,768]{1,0:T(8,128)(2,1)S(1)} collective-permute-done((bf16[256,768]{1,0:T(8,128)(2,1)}, bf16[256,768]{1,0:T(8,128)(2,1)S(1)}, u32[]{:S(2)}, u32[]{:S(2)}) %collective-permute-start.2) | collective-permute-done | bytes 393248 | tf_op jit(solution)/shard_map/ppermute | solution.py:27
  77.2 0.8 copy-done.1
  78.0 8.0 %epilogue.1.packed_ref = bf16[8,24576]{1,0:T(8,128)(2,1)} custom-call(bf16[256,8192]{1,0:T(8,128)(2,1)} %bitcast.11, f32[256,1]{1,0:T(8,128)} %get-tuple-element.17.inv_ref, bf16[1,8192]{1,0:T(2,128)(2,1)} %reshape.16.scale_ref, bf16[16,8192]{1,0:T(8,128)(2,1)} %copy-done, f32[8,256]{1,0:T(8,128)} %get-tuple-element.20.dq_mid_ref, ...), custom_call_target="tpu_custom_call" | custom-call | flops 167772160 | bytes 4194304 | tf_op jit(solution)/shard_map/epilogue/pallas_call | solution.py:283
  86.0 22.1 %reduced.1 = (f32[8,8192]{1,0:T(8,128)}, f32[8,6144]{1,0:T(8,128)}, f32[8,8192]{1,0:T(8,128)}, f32[8,768]{1,0:T(8,128)}, f32[8,1024]{1,0:T(8,128)}) custom-call(bf16[8,24576]{1,0:T(8,128)(2,1)} %epilogue.1.packed_ref), custom_call_target="tpu_custom_call" | custom-call | tf_op jit(solution)/shard_map/reduced/pallas_call | solution.py:432
  108.1 1.4 %copy.19 = f32[1,8,8,128]{3,1,2,0:T(8,128)} copy(f32[1,8,8,128]{3,2,1,0:T(8,128)} %bitcast.16) | data formatting | bytes 65536
  109.4 1.7 %copy.25 = f32[8,8192]{1,0:T(8,128)} copy(f32[8,8192]{1,0:T(8,128)} %get-tuple-element.34) | data formatting | bytes 524288
  111.1 1.6 %copy.26 = f32[8,6144]{1,0:T(8,128)} copy(f32[8,6144]{1,0:T(8,128)} %get-tuple-element.35) | data formatting | bytes 393216
  112.7 1.7 %copy.27 = f32[8,8192]{1,0:T(8,128)} copy(f32[8,8192]{1,0:T(8,128)} %get-tuple-element.36) | data formatting | bytes 524288
  114.4 1.3 %copy.28 = f32[8,768]{1,0:T(8,128)} copy(f32[8,768]{1,0:T(8,128)} %get-tuple-element.37) | data formatting | bytes 49152
  (3 shorter events, 0.0 us)
Async XLA Ops:
  0.6 16.1 %collective-permute-start = (bf16[256,768]{1,0:T(8,128)(2,1)}, bf16[256,768]{1,0:T(8,128)(2,1)S(1)}, u32[]{:S(2)}, u32[]{:S(2)}) collective-permute-start(bf16[256,768]{1,0:T(8,128)(2,1)} %bitcast.19), channel_id=1, source_target_pairs={{24,0},{0,8},{8,16},{16,24},{25,1},{1,9},{9,17},{17,25},{26,2},{2,... | collective-permute-start | bytes 1179656 | tf_op jit(solution)/shard_map/ppermute | solution.py:27
  6.8 0.7 copy-start
  13.8 11.7 %collective-permute-start.1 = (bf16[256,768]{1,0:T(8,128)(2,1)}, bf16[256,768]{1,0:T(8,128)(2,1)S(1)}, u32[]{:S(2)}, u32[]{:S(2)}) collective-permute-start(bf16[256,768]{1,0:T(8,128)(2,1)} %get-tuple-element.18.value_ref), channel_id=1, source_target_pairs={{24,0},{0,8},{8,16},{16,24},{25,1},{1,9},{9,17},{17,25},{26,2},{2,... | collective-permute-start | bytes 1179656 | tf_op jit(solution)/shard_map/ppermute | solution.py:27
  16.8 8.7 %copy-start.2 = (bf16[256,768]{1,0:T(8,128)(2,1)}, bf16[256,768]{1,0:T(8,128)(2,1)S(1)}, u32[]{:S(2)}) copy-start(bf16[256,768]{1,0:T(8,128)(2,1)S(1)} %collective-permute-done.prior_key_ref) | copy-start | bytes 1179652
  25.5 0.7 copy-start.3
  67.2 10.0 %collective-permute-start.2 = (bf16[256,768]{1,0:T(8,128)(2,1)}, bf16[256,768]{1,0:T(8,128)(2,1)S(1)}, u32[]{:S(2)}, u32[]{:S(2)}) collective-permute-start(bf16[256,768]{1,0:T(8,128)(2,1)} %get-tuple-element.22), channel_id=1, source_target_pairs={{8,0},{16,8},{24,16},{0,24},{9,1},{17,9},{25,17},{1,25},{10,2},{18... | collective-permute-start | bytes 1179656 | tf_op jit(solution)/shard_map/ppermute | solution.py:27
  77.2 0.8 copy-start.1

commit v2 on v1

v2 whole, which is shorter than its diff:
```python
import functools
import math

import jax
import jax.numpy as jnp
from jax import lax
from jax.experimental import pallas as pl
from jax.experimental.pallas import tpu as pltpu
from jax.sharding import PartitionSpec as P

HEAD_SIZE = 128
CORES = 2
LANES = 128


EPS = 1e-05
ADAPTER_SCALE = 2.0
F32 = jnp.float32
BF16 = jnp.bfloat16
NT = (((1,), (1,)), ((), ()))
NN = (((1,), (0,)), ((), ()))


def from_behind(block, axis, distance):
    devices = range(lax.axis_size(axis))
    route = [((i - distance) % len(devices), i) for i in devices]
    return lax.ppermute(block, axis, route)


def dot(left, right, dims):
    return lax.dot_general(left, right, dims, preferred_element_type=F32)


def scaled(block, scale_ref, first, chunks):
    scale = scale_ref[pl.ds(first, chunks), :].astype(F32)
    return jnp.concatenate(
        [
            (block[:, i * LANES : (i + 1) * LANES] * scale[i : i + 1]).astype(BF16)
            for i in range(chunks)
        ],
        axis=1,
    )


def flipped(columns, start, count):
    rows = lax.broadcasted_iota(jnp.int32, (count, columns.shape[1]), 0)
    cols = lax.broadcasted_iota(jnp.int32, (count, columns.shape[1]), 1)
    pick = jnp.where(rows + start == cols, ADAPTER_SCALE, 0.0).astype(BF16)
    return dot(pick, columns, NT).astype(BF16)


def prologue_kernel(
    heads_ref,
    x_ref,
    scale_ref,
    qdown_ref,
    vdown_ref,
    fv_ref,
    vup_ref,
    inv_ref,
    qmid_ref,
    vmid_ref,
    value_ref,
    given_ref,
):
    width = x_ref.shape[1]
    hidden = x_ref[...].astype(F32)
    inverse = lax.rsqrt(jnp.sum(hidden * hidden, axis=-1, keepdims=True) * (1.0 / width) + EPS)
    inv_ref[...] = inverse
    normed = scaled(hidden * inverse, scale_ref, 0, width // LANES)
    qmid_ref[...] = dot(normed, qdown_ref[...], NT).astype(BF16)
    value_mid = dot(normed, vdown_ref[...], NT).astype(BF16)
    vmid_ref[...] = value_mid
    value_ref[...] = (
        fv_ref[...].astype(F32) + dot((value_mid * ADAPTER_SCALE).astype(BF16), vup_ref[...], NN)
    ).astype(BF16)
    half = given_ref.shape[1] // HEAD_SIZE
    for i in range(half):
        at = pl.multiple_of(heads_ref[half + i] * HEAD_SIZE, HEAD_SIZE)
        given_ref[:, i * HEAD_SIZE : (i + 1) * HEAD_SIZE] = value_ref[:, pl.ds(at, HEAD_SIZE)]


def prologue(heads, x, scale, qdown, vdown, frozen_values, vup, steps):
    rows, width = x.shape
    block = rows // steps
    kv = frozen_values.shape[1]
    rank = qdown.shape[0]
    whole = lambda i, heads: (0, 0)
    by_rows = lambda i, heads: (i, 0)
    return pl.pallas_call(
        prologue_kernel,
        grid_spec=pltpu.PrefetchScalarGridSpec(
            num_scalar_prefetch=1,
            grid=(steps,),
            in_specs=[
                pl.BlockSpec((block, width), by_rows),
                pl.BlockSpec(scale.shape, whole),
                pl.BlockSpec(qdown.shape, whole),
                pl.BlockSpec(vdown.shape, whole),
                pl.BlockSpec((block, kv), by_rows),
                pl.BlockSpec(vup.shape, whole),
            ],
            out_specs=[
                pl.BlockSpec((block, 1), by_rows),
                pl.BlockSpec((block, rank), by_rows),
                pl.BlockSpec((block, rank), by_rows),
                pl.BlockSpec((block, kv), by_rows),
                pl.BlockSpec((block, kv // 2), by_rows),
            ],
        ),
        out_shape=[
            jax.ShapeDtypeStruct((rows, 1), F32),
            jax.ShapeDtypeStruct((rows, rank), BF16),
            jax.ShapeDtypeStruct((rows, rank), BF16),
            jax.ShapeDtypeStruct((rows, kv), BF16),
            jax.ShapeDtypeStruct((rows, kv // 2), BF16),
        ],
        cost_estimate=pl.CostEstimate(
            flops=40 * rows * width, bytes_accessed=2 * rows * width, transcendentals=0
        ),
        name="prologue",
    )(heads, x, scale, qdown, vdown, frozen_values, vup)


def attention_kernel(has_start, with_prior, heads_ref, *refs):
    refs = list(refs)
    fq_ref, grad_ref, key_ref, value_ref, mid_ref, up_ref = refs[:6]
    refs = refs[6:]
    if has_start:
        start_ref = refs.pop(0)
    if with_prior:
        prior_key_ref, prior_value_ref = refs.pop(0), refs.pop(0)
    dv_ref, qb_ref, dq_mid_ref = refs[:3]
    rows = fq_ref.shape[0]
    heads = fq_ref.shape[1] // HEAD_SIZE
    rank = up_ref.shape[0]
    factor = 1.0 / math.sqrt(HEAD_SIZE)

    @pl.when(pl.program_id(0) == 0)
    def _():
        dq_mid_ref[...] = start_ref[...] if has_start else jnp.zeros_like(dq_mid_ref)

    keys = key_ref[...]
    values = value_ref[...]
    if with_prior:
        keys = jnp.concatenate([keys, prior_key_ref[...]], axis=0)
        values = jnp.concatenate([values, prior_value_ref[...]], axis=0)
    keys_t = keys.T
    query_mid = (mid_ref[...] * ADAPTER_SCALE).astype(BF16)
    mid_t = flipped(mid_ref[...], 0, rank)
    key_pos = lax.broadcasted_iota(jnp.int32, (rows, rows), 0)
    query_pos = lax.broadcasted_iota(jnp.int32, (rows, rows), 1)
    causal = key_pos <= query_pos
    dv = None
    dq_mid = dq_mid_ref[...]
    for j in range(heads):
        cols = slice(j * HEAD_SIZE, (j + 1) * HEAD_SIZE)
        up = up_ref[:, cols]
        query = (fq_ref[:, cols].astype(F32) + dot(query_mid, up, NN)).astype(BF16)
        grad = grad_ref[:, cols]
        scores = dot(keys, query, NT)
        own = jnp.where(causal, scores[:rows], -jnp.inf)
        scores = jnp.concatenate([own, scores[rows:]], axis=0) if with_prior else own
        top = jnp.max(scores, axis=0, keepdims=True)
        exponent = jnp.exp2((scores - top) * (factor * math.log2(math.e)))
        probs = exponent * (1.0 / jnp.sum(exponent, axis=0, keepdims=True))
        weights = probs.astype(BF16)
        dprob = dot(values, grad, NT)
        delta = jnp.sum(weights.astype(F32) * dprob, axis=0, keepdims=True)
        dscore = (probs * (dprob - delta)).astype(BF16)
        term = dot(weights, grad, NN)
        dv = term if dv is None else dv + term
        dquery = (dot(keys_t, dscore, NN) * factor).astype(BF16)
        qb_ref[:, cols] = dot(mid_t, dquery, NT)
        dq_mid = dq_mid + dot(up, dquery, NN)
    dq_mid_ref[...] = dq_mid
    dv_ref[...] = dv[:rows]
    if with_prior:
        refs[3][...] = dv[rows:].astype(BF16)


def attention(first, count, heads, fq, grads, keys, values, mid, up, start, prior):
    rows, queries = fq.shape
    kv_heads = keys.shape[1] // HEAD_SIZE
    wide = queries // kv_heads
    rank = up.shape[0]
    by_head = lambda i, heads: (0, heads[first + i])
    by_slot = lambda i, heads: (0, i)
    whole = lambda i, heads: (0, 0)
    narrow = pl.BlockSpec((rows, HEAD_SIZE), by_head)
    broad = pl.BlockSpec((rows, wide), by_head)
    slot = pl.BlockSpec((rows, HEAD_SIZE), by_slot)
    operands = [fq, grads, keys, values, mid, up]
    in_specs = [
        broad,
        broad,
        narrow,
        narrow,
        pl.BlockSpec(mid.shape, whole),
        pl.BlockSpec((rank, wide), by_head),
    ]
    out_specs = [
        slot,
        pl.BlockSpec((rank, wide), by_slot),
        pl.BlockSpec((rank, rows), whole),
    ]
    out_shape = [
        jax.ShapeDtypeStruct((rows, count * HEAD_SIZE), F32),
        jax.ShapeDtypeStruct((rank, count * wide), F32),
        jax.ShapeDtypeStruct((rank, rows), F32),
    ]
    if start is not None:
        operands.append(start)
        in_specs.append(pl.BlockSpec(start.shape, whole))
    if prior is not None:
        operands += list(prior)
        in_specs += [narrow, slot]
        out_specs.append(slot)
        out_shape.append(jax.ShapeDtypeStruct((rows, count * HEAD_SIZE), BF16))
    return pl.pallas_call(
        functools.partial(attention_kernel, start is not None, prior is not None),
        grid_spec=pltpu.PrefetchScalarGridSpec(
            num_scalar_prefetch=1, grid=(count,), in_specs=in_specs, out_specs=out_specs
        ),
        out_shape=out_shape,
        cost_estimate=pl.CostEstimate(
            flops=count * 24 * rows * rows * wide,
            bytes_accessed=count * 4 * rows * wide,
            transcendentals=0,
        ),
        name="attention",
    )(heads, *operands)


def epilogue_kernel(
    counts,
    heads_ref,
    x_ref,
    inv_ref,
    scale_ref,
    qdown_ref,
    vdown_ref,
    dq_mid_ref,
    handed_ref,
    vup_ref,
    vmid_ref,
    *refs,
):
    dv_refs, qb_refs = refs[: len(counts)], refs[len(counts) : 2 * len(counts)]
    packed_ref, inner_ref, gain_ref = refs[2 * len(counts) :]
    step = pl.program_id(0)
    block = x_ref.shape[1]
    rank = vup_ref.shape[0]
    full = gain_ref.shape[0] * block
    kv = vup_ref.shape[1]
    half = handed_ref.shape[1] // HEAD_SIZE
    wide = qb_refs[0].shape[1] // counts[0][1]
    queries = kv // HEAD_SIZE * wide
    base = 2 * full + queries

    @pl.when(step == 0)
    def _():
        mid_t = flipped(vmid_ref[...], 0, rank)
        dv_mid = jnp.zeros(dq_mid_ref.shape, F32)
        for (first, count), dv_ref, qb_ref in zip(counts, dv_refs, qb_refs):
            for i in range(count):
                cols = slice(i * HEAD_SIZE, (i + 1) * HEAD_SIZE)
                dv = dv_ref[:, cols]
                if first + i >= half:
                    given = first + i - half
                    other = handed_ref[:, given * HEAD_SIZE : (given + 1) * HEAD_SIZE]
                    dv = dv + other.astype(F32)
                dv = dv.astype(BF16)
                head = heads_ref[first + i]
                at = pl.multiple_of(head * HEAD_SIZE, HEAD_SIZE)
                dv_mid = dv_mid + dot(vup_ref[:, pl.ds(at, HEAD_SIZE)], dv, NT)
                at = pl.multiple_of(base + head * HEAD_SIZE, HEAD_SIZE)
                packed_ref[:, pl.ds(at, HEAD_SIZE)] = dot(mid_t, dv, NN).astype(BF16)
                at = pl.multiple_of(2 * full + head * wide, HEAD_SIZE)
                packed_ref[:, pl.ds(at, wide)] = qb_ref[:, i * wide : (i + 1) * wide].astype(BF16)
        inner_ref[...] = (
            ADAPTER_SCALE * jnp.concatenate([dq_mid_ref[...], dv_mid], axis=0)
        ).astype(BF16)
        gain_ref[...] = jnp.zeros_like(gain_ref)
        used = base + kv + block
        if used < packed_ref.shape[1]:
            packed_ref[:, used:] = jnp.zeros((rank, packed_ref.shape[1] - used), BF16)

    inner = inner_ref[...]
    unit = x_ref[...].astype(F32) * inv_ref[...]
    normed = scaled(unit, scale_ref, 0, block // LANES)
    raw = dot(inner, normed, NN).astype(BF16)
    at = pl.multiple_of(step * block, block)
    packed_ref[:, pl.ds(at, block)] = raw[:rank]
    packed_ref[:, pl.ds(at + full, block)] = raw[rank:]
    spread = dot(inner, unit.astype(BF16), NN)
    gain = jnp.sum(
        qdown_ref[...].astype(F32) * spread[:rank] + vdown_ref[...].astype(F32) * spread[rank:],
        axis=0,
        keepdims=True,
    )
    row = lax.broadcasted_iota(jnp.int32, gain_ref.shape, 0)
    gain_ref[...] = jnp.where(row == step, gain, gain_ref[...])

    @pl.when(step == pl.num_programs(0) - 1)
    def _():
        packed_ref[:, base + kv : base + kv + block] = gain_ref[...].astype(BF16)


def epilogue(heads, counts, x, inverse, scale, qdown, vdown, dq_mid, handed, vup, vmid, dvs, qbs, total):
    rows, width = x.shape
    rank = vup.shape[0]
    block = width // rank
    whole = lambda j, heads: (0, 0)
    by_cols = lambda j, heads: (0, j)
    kept = lambda a: pl.BlockSpec(a.shape, whole)
    return pl.pallas_call(
        functools.partial(epilogue_kernel, counts),
        grid_spec=pltpu.PrefetchScalarGridSpec(
            num_scalar_prefetch=1,
            grid=(rank,),
            in_specs=[
                pl.BlockSpec((rows, block), by_cols),
                kept(inverse),
                pl.BlockSpec((block // LANES, LANES), lambda j, heads: (j, 0)),
                pl.BlockSpec((rank, block), by_cols),
                pl.BlockSpec((rank, block), by_cols),
                kept(dq_mid),
                kept(handed),
                kept(vup),
                kept(vmid),
            ]
            + [kept(a) for a in (*dvs, *qbs)],
            out_specs=pl.BlockSpec((rank, total), whole),
            scratch_shapes=[
                pltpu.VMEM((2 * rank, rows), BF16),
                pltpu.VMEM((rank, block), F32),
            ],
        ),
        out_shape=jax.ShapeDtypeStruct((rank, total), BF16),
        cost_estimate=pl.CostEstimate(
            flops=80 * rows * width, bytes_accessed=2 * rows * width, transcendentals=0
        ),
        name="epilogue",
    )(heads, x, inverse, scale, qdown, vdown, dq_mid, handed, vup, vmid, *dvs, *qbs)


def finish_kernel(limit, full_ref, qa_ref, qb_ref, va_ref, vb_ref, gain_ref):
    sums = full_ref[...].astype(F32)
    squares = jnp.sum(jnp.sum(sums * sums, axis=1, keepdims=True), axis=0, keepdims=True)
    scale = jnp.minimum(1.0, limit / jnp.sqrt(squares))
    at = 0
    for out in (qa_ref, va_ref, qb_ref, vb_ref):
        out[...] = full_ref[:, at : at + out.shape[1]].astype(F32) * scale
        at += out.shape[1]
    rank = full_ref.shape[0]
    chunks = gain_ref.shape[0] // rank
    for c in range(chunks):
        piece = full_ref[:, at + c * LANES : at + (c + 1) * LANES].astype(F32) * scale
        gain_ref[pl.ds(c, rank, stride=chunks), :] = piece


def finished(full, limit, widths, width):
    rank = full.shape[0]
    vmem = pl.BlockSpec(memory_space=pltpu.VMEM)
    return pl.pallas_call(
        functools.partial(finish_kernel, limit),
        in_specs=[vmem],
        out_specs=[vmem] * (len(widths) + 1),
        out_shape=[jax.ShapeDtypeStruct((rank, w), F32) for w in widths]
        + [jax.ShapeDtypeStruct((width // LANES, LANES), F32)],
        name="finished",
    )(full)


def reduce_kernel(
    seqs,
    planes,
    packed_ref,
    full,
    parts,
    column,
    send_one,
    recv_one,
    send_two,
    recv_two,
    send_three,
    recv_three,
):
    group = seqs * CORES
    piece = full.shape[1] // group
    place = lax.axis_index("dp")
    plane = place // CORES
    me = lax.axis_index("seq") * CORES + place % CORES

    def in_group(k):
        peer = lax.rem(me + k, group)
        return peer, {"seq": peer // CORES, "dp": plane * CORES + peer % CORES}

    def in_column(k):
        return {"dp": lax.rem(plane + k, planes) * CORES + place % CORES}

    def span(index):
        return pl.ds(pl.multiple_of(index * piece, piece), piece)

    barrier = pltpu.get_barrier_semaphore()
    for k in range(1, group):
        pl.semaphore_signal(
            barrier, inc=1, device_id=in_group(k)[1], device_id_type=pl.DeviceIdType.MESH
        )
    for k in range(1, planes):
        pl.semaphore_signal(
            barrier, inc=1, device_id=in_column(k), device_id_type=pl.DeviceIdType.MESH
        )
    pl.semaphore_wait(barrier, group + planes - 2)

    def remote(source, target, send, recv, device):
        copy = pltpu.make_async_remote_copy(
            src_ref=source,
            dst_ref=target,
            send_sem=send,
            recv_sem=recv,
            device_id=device,
            device_id_type=pl.DeviceIdType.MESH,
        )
        copy.start()
        return copy

    first = []
    for k in range(1, group):
        peer, device = in_group(k)
        first.append(
            remote(
                packed_ref.at[:, span(peer)],
                parts.at[k - 1],
                send_one.at[k - 1],
                recv_one.at[k - 1],
                device,
            )
        )
    total = packed_ref[:, span(me)].astype(F32)
    for k in range(1, group):
        first[k - 1].wait_recv()
        total = total + parts[k - 1].astype(F32)
    column[plane] = total.astype(BF16)
    second = [
        remote(
            column.at[plane],
            column.at[plane],
            send_two.at[k - 1],
            recv_two.at[k - 1],
            in_column(k),
        )
        for k in range(1, planes)
    ]
    for copy in second:
        copy.wait_recv()
    total = column[0].astype(F32)
    for i in range(1, planes):
        total = total + column[i].astype(F32)
    full[:, span(me)] = total.astype(BF16)
    third = [
        remote(
            full.at[:, span(me)],
            full.at[:, span(me)],
            send_three.at[k - 1],
            recv_three.at[k - 1],
            in_group(k)[1],
        )
        for k in range(1, group)
    ]
    for copy in third:
        copy.wait_recv()
    for copy in first + second + third:
        copy.wait_send()


def reduced(packed, seqs, planes):
    rank, total = packed.shape
    group = seqs * CORES
    piece = total // group
    vmem = pl.BlockSpec(memory_space=pltpu.VMEM)
    dma = pltpu.SemaphoreType.DMA
    return pl.pallas_call(
        functools.partial(reduce_kernel, seqs, planes),
        in_specs=[vmem],
        out_specs=vmem,
        out_shape=jax.ShapeDtypeStruct((rank, total), BF16),
        scratch_shapes=[
            pltpu.VMEM((group - 1, rank, piece), BF16),
            pltpu.VMEM((planes, rank, piece), BF16),
            dma((group - 1,)),
            dma((group - 1,)),
            dma((max(planes - 1, 1),)),
            dma((max(planes - 1, 1),)),
            dma((group - 1,)),
            dma((group - 1,)),
        ],
        compiler_params=pltpu.CompilerParams(collective_id=0, has_side_effects=True),
        name="reduced",
    )(packed)


def shards(
    layer_input,
    frozen_queries,
    frozen_keys,
    frozen_values,
    output_gradient,
    norm_scale_vector,
    query_down_weight,
    query_up_weight,
    value_down_weight,
    value_up_weight,
    head_ordering,
):
    seqs = lax.axis_size("seq")
    planes = lax.axis_size("dp") // CORES
    rank, width = query_down_weight.shape
    queries = query_up_weight.shape[1]
    kv = value_up_weight.shape[1]
    half = head_ordering.shape[0] // 2
    odd = lax.axis_index("seq") % 2 == 1
    heads = jnp.where(odd, jnp.roll(head_ordering, -half), head_ordering)
    scale = norm_scale_vector.reshape(width // LANES, LANES)
    x, fq, grads, keys = layer_input[0], frozen_queries[0], output_gradient[0], frozen_keys[0]
    prior_keys = from_behind(keys, "seq", 1)
    inverse, qmid, vmid, values, given = prologue(
        heads, x, scale, query_down_weight, value_down_weight, frozen_values[0], value_up_weight, 4
    )
    prior_values = from_behind(given, "seq", 1)
    counts = ((half, half - 1), (0, half), (2 * half - 1, 1))
    attend = functools.partial(attention, heads=heads, fq=fq, grads=grads, keys=keys)
    attend = functools.partial(attend, values=values, mid=qmid, up=query_up_weight)
    dv_a, qb_a, dq_mid = attend(*counts[0], start=None, prior=None)
    dv_b, qb_b, dq_mid, dv_prior = attend(
        *counts[1], start=dq_mid, prior=(prior_keys, prior_values)
    )
    handed = from_behind(dv_prior, "seq", -1)
    dv_c, qb_c, dq_mid = attend(*counts[2], start=dq_mid, prior=None)
    used = 2 * width + queries + kv + width // rank
    unit = seqs * CORES * LANES
    total = -(-used // unit) * unit
    packed = epilogue(
        heads,
        counts,
        x,
        inverse,
        scale,
        query_down_weight,
        value_down_weight,
        dq_mid,
        handed,
        value_up_weight,
        vmid,
        (dv_a, dv_b, dv_c),
        (qb_a, qb_b, qb_c),
        total,
    )
    limit = math.sqrt(rank * (2 * width + queries + kv) + width)
    qa, gqb, va, vb, gain = finished(
        reduced(packed, seqs, planes), limit, (width, queries, width, kv), width
    )
    return (qa, gqb, va, vb, gain.reshape(width))


def solution(mesh):
    placed = (
        P("dp", "seq", None),
        P("dp", "seq", None),
        P("dp", "seq", None),
        P("dp", "seq", None),
        P("dp", "seq", None),
        P(),
        P(),
        P(),
        P(),
        P(),
        P(),
    )
    return jax.shard_map(
        shards, mesh=mesh, in_specs=placed, out_specs=(P(), P(), P(), P(), P()), check_vma=False
    )
```

time: 117 us -> 95.7 us (0.82)
  waiting for transfers between devices: 18.3 us -> 0.01 us
  local copies, waits for them, and re-layouts: 14.6 us -> 2.27 us
  Pallas kernels: 77.3 us -> 84.8 us
  starting transfers between devices: 4.93 us -> 6.18 us
  other arithmetic: 0 us -> 1.24 us
    ppermute x3, waiting for transfers between devices: 18.3 us -> 0.01 us  [from_behind(): return lax.ppermute(block, axis, route)]
    unnamed x14 -> x6, local copies, waits for them, and re-layouts: 10.8 us -> 1.47 us
    pallas_call x4 -> x7, Pallas kernels: 77.3 us -> 84.8 us  [the longest x3 45.5 us: attention(): pl.pallas_call(functools.partial(attention_kernel, start is not None, pri...]
    pallas_call x1 -> x0, local copies, waits for them, and re-layouts: 1.51 us -> none  [prologue(): pl.pallas_call(prologue_kernel, grid=(steps,), in_specs=[pl.BlockSpec((bl...]
    reshape x1 -> x0, local copies, waits for them, and re-layouts: 1.35 us -> none  [shards(): scale = norm_scale_vector.reshape(1, width)]
    ppermute x3, starting transfers between devices: 4.93 us -> 6.18 us  [from_behind(): return lax.ppermute(block, axis, route)]
    select_n x0 -> x1, other arithmetic: none -> 1.24 us  [shards(): heads = jnp.where(odd, jnp.roll(head_ordering, -half), head_ordering)]
  transfers between devices with their start and end apart: 3 -> 3, of which waited for: 2 -> 0; matrix products, arithmetic and copies ran while one was open for 4% -> 2% of each run, Pallas kernels for 5% -> 30%
where the time goes in v2:
time: 95.7 us; the launch traced here: 95.2 us
  Pallas kernels  84.8 us (89%)
  starting transfers between devices  6.18 us (6%)
  local copies, waits for them, and re-layouts  2.27 us (2%)
  other arithmetic  1.24 us (1%)
    pallas_call x3, Pallas kernels, attention(): pl.pallas_call(functools.partial(attention_kernel, start is not None, pri...  45.5 us
    pallas_call x1, Pallas kernels, reduced(): pl.pallas_call(functools.partial(reduce_kernel, seqs, planes), in_specs=[...  20.9 us
    pallas_call x1, Pallas kernels, epilogue(): pl.pallas_call(functools.partial(epilogue_kernel, counts), grid_spec=pltp...  8.72 us
    pallas_call x1, Pallas kernels, prologue(): pl.pallas_call(prologue_kernel, grid_spec=pltpu.PrefetchScalarGridSpec(nu...  7.48 us
    ppermute x3, starting transfers between devices, from_behind(): return lax.ppermute(block, axis, route)  6.18 us
    pallas_call x1, Pallas kernels, finished(): pl.pallas_call(functools.partial(finish_kernel, limit), in_specs=[vmem],...  2.18 us
  transfers between devices with their start and end apart: 3, of which 0 were waited for; matrix products, arithmetic and copies ran while one was open for 2% of the time, Pallas kernels for 30%

profile of v2, /device:TPU:0, one launch (start us, length us, event | category | flops | bytes accessed | tf_op | source)
XLA Modules:
  0.0 95.2 jit_solution(4383657131102253922)
XLA Ops:
  0.6 3.0 %collective-permute-start = (bf16[256,768]{1,0:T(8,128)(2,1)}, bf16[256,768]{1,0:T(8,128)(2,1)S(1)}, u32[]{:S(2)}, u32[]{:S(2)}) collective-permute-start(bf16[256,768]{1,0:T(8,128)(2,1)} %bitcast.16), channel_id=1, source_target_pairs={{24,0},{0,8},{8,16},{16,24},{25,1},{1,9},{9,17},{17,25},{26,2},{2,... | collective-permute-start | bytes 1179656 | tf_op jit(solution)/shard_map/ppermute | solution.py:27
  3.6 0.8 fusion
  4.5 1.2 %broadcast_select_fusion.heads_ref = s32[6]{0:T(128)} fusion(s32[6]{0:T(128)} %param.21, pred[]{:T(512)S(6)} %eq.5, s32[3]{0:T(128)S(1)} %get-tuple-element.46, s32[3]{0:T(128)S(1)} %get-tuple-element.45), kind=kLoop, calls=%fused_computation | loop fusion | flops 12 | bytes 73 | tf_op jit(solution)/shard_map/jit(_where)/select_n | solution.py:524
  5.7 7.5 %prologue.1 = (f32[256,1]{1,0:T(8,128)}, bf16[256,8]{1,0:T(8,128)(2,1)}, bf16[256,8]{1,0:T(8,128)(2,1)}, bf16[256,768]{1,0:T(8,128)(2,1)}, bf16[256,384]{1,0:T(8,128)(2,1)}) custom-call(s32[6]{0:T(128)} %broadcast_select_fusion.heads_ref, bf16[256,8192]{1,0:T(8,128)(2,1)} %bitcast.7, bf16[64,128]{1,0:T(8,128)(2,1)} %bitcast.20, bf16[8,8192]{1,0:T(8,128)(2,1)} %qdown_ref.3, ...), custom_call_target="tpu_custom_call" | custom-call | flops 83886080 | bytes 4194304 | tf_op jit(solution)/shard_map/prologue/pallas_call | solution.py:90
  13.2 0.8 collective-permute-start.1
  14.0 13.1 %attention.3 = (f32[256,256]{1,0:T(8,128)}, f32[8,2048]{1,0:T(8,128)}, f32[8,256]{1,0:T(8,128)}) custom-call(s32[6]{0:T(128)} %broadcast_select_fusion.heads_ref, bf16[256,6144]{1,0:T(8,128)(2,1)} %bitcast.9, bf16[256,6144]{1,0:T(8,128)(2,1)} %bitcast.12, bf16[256,768]{1,0:T(8,128)(2,1)} %bitcast.17, bf16[256,768]{1,0:T(8,128)(2,1)} %get-tuple-element.26.refs_3_, ...), custom_call_target="tpu_custom_call" | custom-call | flops 3221225472 | bytes 2097152 | tf_op jit(solution)/shard_map/attention/pallas_call | solution.py:220
  27.1 0.0 collective-permute-done.1.refs_8_
  27.2 0.0 copy-start.2
  27.2 0.0 collective-permute-done.refs_7_
  27.2 0.0 copy-start.1
  27.2 0.6 copy-done.2
  27.8 0.1 copy-done.1
  28.0 24.7 %attention.4 = (f32[256,384]{1,0:T(8,128)}, f32[8,3072]{1,0:T(8,128)}, f32[8,256]{1,0:T(8,128)}, bf16[256,384]{1,0:T(8,128)(2,1)}) custom-call(s32[6]{0:T(128)} %broadcast_select_fusion.heads_ref, bf16[256,6144]{1,0:T(8,128)(2,1)} %bitcast.10, bf16[256,6144]{1,0:T(8,128)(2,1)} %bitcast.13, bf16[256,768]{1,0:T(8,128)(2,1)} %bitcast.18, ...), custom_call_target="tpu_custom_call" | custom-call | flops 4831838208 | bytes 3145728 | tf_op jit(solution)/shard_map/attention/pallas_call | solution.py:220
  52.7 2.3 %collective-permute-start.2 = (bf16[256,384]{1,0:T(8,128)(2,1)}, bf16[256,384]{1,0:T(8,128)(2,1)S(1)}, u32[]{:S(2)}, u32[]{:S(2)}) collective-permute-start(bf16[256,384]{1,0:T(8,128)(2,1)} %get-tuple-element.32), channel_id=1, source_target_pairs={{8,0},{16,8},{24,16},{0,24},{9,1},{17,9},{25,17},{1,25},{10,2},{18... | collective-permute-start | bytes 589832 | tf_op jit(solution)/shard_map/ppermute | solution.py:27
  55.0 7.7 %attention.5 = (f32[256,128]{1,0:T(8,128)}, f32[8,1024]{1,0:T(8,128)}, f32[8,256]{1,0:T(8,128)}) custom-call(s32[6]{0:T(128)} %broadcast_select_fusion.heads_ref, bf16[256,6144]{1,0:T(8,128)(2,1)} %bitcast.11, bf16[256,6144]{1,0:T(8,128)(2,1)} %bitcast.14, bf16[256,768]{1,0:T(8,128)(2,1)} %bitcast.19, bf16[256,768]{1,0:T(8,128)(2,1)} %get-tuple-element.26.refs_3_, ...), custom_call_target="tpu_custom_call" | custom-call | flops 1610612736 | bytes 1048576 | tf_op jit(solution)/shard_map/attention/pallas_call | solution.py:220
  62.7 0.0 collective-permute-done.2.handed_ref
  62.7 0.0 copy-start
  62.7 0.7 copy-done
  63.4 8.7 %epilogue.1.packed_ref = bf16[8,24576]{1,0:T(8,128)(2,1)} custom-call(s32[6]{0:T(128)} %broadcast_select_fusion.heads_ref, bf16[256,8192]{1,0:T(8,128)(2,1)} %bitcast.8, f32[256,1]{1,0:T(8,128)} %get-tuple-element.25.inv_ref, bf16[64,128]{1,0:T(8,128)(2,1)} %bitcast.21, bf16[8,8192]{1,0:T(8,128)(2,1)} %qdown_ref.3, bf16[8,8192]{1,0:T(8,128)(2,1)} %vdown_ref.3, ...), custom_call_target="tpu_custom_call" | custom-call | flops 167772160 | bytes 4194304 | tf_op jit(solution)/shard_map/epilogue/pallas_call | solution.py:317
  72.1 20.9 %reduced.1.full_ref = bf16[8,24576]{1,0:T(8,128)(2,1)} custom-call(bf16[8,24576]{1,0:T(8,128)(2,1)} %epilogue.1.packed_ref), custom_call_target="tpu_custom_call" | custom-call | tf_op jit(solution)/shard_map/reduced/pallas_call | solution.py:484
  93.0 2.2 %finished.1 = (f32[8,8192]{1,0:T(8,128)}, f32[8,6144]{1,0:T(8,128)}, f32[8,8192]{1,0:T(8,128)}, f32[8,768]{1,0:T(8,128)}, f32[64,128]{1,0:T(8,128)}) custom-call(bf16[8,24576]{1,0:T(8,128)(2,1)} %reduced.1.full_ref), custom_call_target="tpu_custom_call" | custom-call | tf_op jit(solution)/shard_map/finished/pallas_call | solution.py:366
Async XLA Ops:
  0.6 26.5 %collective-permute-start = (bf16[256,768]{1,0:T(8,128)(2,1)}, bf16[256,768]{1,0:T(8,128)(2,1)S(1)}, u32[]{:S(2)}, u32[]{:S(2)}) collective-permute-start(bf16[256,768]{1,0:T(8,128)(2,1)} %bitcast.16), channel_id=1, source_target_pairs={{24,0},{0,8},{8,16},{16,24},{25,1},{1,9},{9,17},{17,25},{26,2},{2,... | collective-permute-start | bytes 1179656 | tf_op jit(solution)/shard_map/ppermute | solution.py:27
  13.2 14.0 %collective-permute-start.1 = (bf16[256,384]{1,0:T(8,128)(2,1)}, bf16[256,384]{1,0:T(8,128)(2,1)S(1)}, u32[]{:S(2)}, u32[]{:S(2)}) collective-permute-start(bf16[256,384]{1,0:T(8,128)(2,1)} %get-tuple-element.29), channel_id=1, source_target_pairs={{24,0},{0,8},{8,16},{16,24},{25,1},{1,9},{9,17},{17,25},{26,2},{2,... | collective-permute-start | bytes 589832 | tf_op jit(solution)/shard_map/ppermute | solution.py:27
  27.2 0.7 copy-start.2
  27.2 0.8 copy-start.1
  52.7 10.1 %collective-permute-start.2 = (bf16[256,384]{1,0:T(8,128)(2,1)}, bf16[256,384]{1,0:T(8,128)(2,1)S(1)}, u32[]{:S(2)}, u32[]{:S(2)}) collective-permute-start(bf16[256,384]{1,0:T(8,128)(2,1)} %get-tuple-element.32), channel_id=1, source_target_pairs={{8,0},{16,8},{24,16},{0,24},{9,1},{17,9},{25,17},{1,25},{10,2},{18... | collective-permute-start | bytes 589832 | tf_op jit(solution)/shard_map/ppermute | solution.py:27
  62.7 0.7 copy-start

commit v3 on v2

--- a/solution.py
+++ b/solution.py
@@ -11,6 +11,7 @@
 HEAD_SIZE = 128
 CORES = 2
 LANES = 128
+TOGETHER = 8
 
 
 EPS = 1e-05
@@ -151,15 +152,24 @@
     key_pos = lax.broadcasted_iota(jnp.int32, (rows, rows), 0)
     query_pos = lax.broadcasted_iota(jnp.int32, (rows, rows), 1)
     causal = key_pos <= query_pos
+    together = math.gcd(heads, TOGETHER)
+    up = up_ref[...]
+    query = (fq_ref[...].astype(F32) + dot(query_mid, up, NN)).astype(BF16)
     dv = None
-    dq_mid = dq_mid_ref[...]
-    for j in range(heads):
-        cols = slice(j * HEAD_SIZE, (j + 1) * HEAD_SIZE)
-        up = up_ref[:, cols]
-        query = (fq_ref[:, cols].astype(F32) + dot(query_mid, up, NN)).astype(BF16)
-        grad = grad_ref[:, cols]
-        scores = dot(keys, query, NT)
-        own = jnp.where(causal, scores[:rows], -jnp.inf)
+    dqueries = []
+    for j in range(0, heads, together):
+        stacked = lambda array: jnp.concatenate(
+            [array[:, i * HEAD_SIZE : (i + 1) * HEAD_SIZE] for i in range(j, j + together)], axis=0
+        )
+        grad = stacked(grad_ref)
+        scores = dot(keys, stacked(query), NT)
+        own = jnp.concatenate(
+            [
+                jnp.where(causal, scores[:rows, i * rows : (i + 1) * rows], -jnp.inf)
+                for i in range(together)
+            ],
+            axis=1,
+        )
         scores = jnp.concatenate([own, scores[rows:]], axis=0) if with_prior else own
         top = jnp.max(scores, axis=0, keepdims=True)
         exponent = jnp.exp2((scores - top) * (factor * math.log2(math.e)))
@@ -171,9 +181,10 @@
         term = dot(weights, grad, NN)
         dv = term if dv is None else dv + term
         dquery = (dot(keys_t, dscore, NN) * factor).astype(BF16)
-        qb_ref[:, cols] = dot(mid_t, dquery, NT)
-        dq_mid = dq_mid + dot(up, dquery, NN)
-    dq_mid_ref[...] = dq_mid
+        dqueries += [dquery[:, i * rows : (i + 1) * rows] for i in range(together)]
+    dquery = jnp.concatenate(dqueries, axis=0)
+    qb_ref[...] = dot(mid_t, dquery, NT)
+    dq_mid_ref[...] += dot(up, dquery, NN)
     dv_ref[...] = dv[:rows]
     if with_prior:
         refs[3][...] = dv[rows:].astype(BF16)

time: 95.7 us -> 76.2 us (0.80)
  Pallas kernels: 84.8 us -> 65.4 us
    pallas_call x3, Pallas kernels: 45.5 us -> 24.2 us  [attention(): pl.pallas_call(functools.partial(attention_kernel, start is not None, pri...]
    pallas_call x1, Pallas kernels: 20.9 us -> 22.7 us  [reduced(): pl.pallas_call(functools.partial(reduce_kernel, seqs, planes), in_specs=[...]
  transfers between devices with their start and end apart: 3 -> 3, of which waited for: 0 -> 1; matrix products, arithmetic and copies ran while one was open for 2% -> 3% of each run, Pallas kernels for 30% -> 25%
where the time goes in v3:
time: 76.2 us; the launch traced here: 75.7 us
  Pallas kernels  65.4 us (86%)
  starting transfers between devices  5.98 us (8%)
  local copies, waits for them, and re-layouts  2.27 us (3%)
  other arithmetic  1.24 us (2%)
    pallas_call x3, Pallas kernels, attention(): pl.pallas_call(functools.partial(attention_kernel, start is not None, pri...  24.2 us
    pallas_call x1, Pallas kernels, reduced(): pl.pallas_call(functools.partial(reduce_kernel, seqs, planes), in_specs=[...  22.7 us
    pallas_call x1, Pallas kernels, epilogue(): pl.pallas_call(functools.partial(epilogue_kernel, counts), grid_spec=pltp...  8.72 us
    pallas_call x1, Pallas kernels, prologue(): pl.pallas_call(prologue_kernel, grid_spec=pltpu.PrefetchScalarGridSpec(nu...  7.48 us
    ppermute x3, starting transfers between devices, from_behind(): return lax.ppermute(block, axis, route)  5.98 us
    pallas_call x1, Pallas kernels, finished(): pl.pallas_call(functools.partial(finish_kernel, limit), in_specs=[vmem],...  2.18 us
  transfers between devices with their start and end apart: 3, of which 1 were waited for; matrix products, arithmetic and copies ran while one was open for 3% of the time, Pallas kernels for 25%

profile of v3, /device:TPU:0, one launch (start us, length us, event | category | flops | bytes accessed | tf_op | source)
XLA Modules:
  0.0 75.7 jit_solution(5376613514482408246)
XLA Ops:
  0.6 3.0 %collective-permute-start = (bf16[256,768]{1,0:T(8,128)(2,1)}, bf16[256,768]{1,0:T(8,128)(2,1)S(1)}, u32[]{:S(2)}, u32[]{:S(2)}) collective-permute-start(bf16[256,768]{1,0:T(8,128)(2,1)} %bitcast.16), channel_id=1, source_target_pairs={{24,0},{0,8},{8,16},{16,24},{25,1},{1,9},{9,17},{17,25},{26,2},{2,... | collective-permute-start | bytes 1179656 | tf_op jit(solution)/shard_map/ppermute | solution.py:28
  3.6 0.8 %fusion = (s32[3]{0:T(128)S(1)}, s32[3]{0:T(128)S(1)}) fusion(s32[6]{0:T(128)} %param.21), kind=kLoop, calls=%fused_computation.1 | loop fusion | bytes 48 | tf_op jit(solution)/shard_map/jit(_roll_static)/slice | solution.py:535
  4.5 1.2 %broadcast_select_fusion.heads_ref = s32[6]{0:T(128)} fusion(s32[6]{0:T(128)} %param.21, pred[]{:T(512)S(6)} %eq.5, s32[3]{0:T(128)S(1)} %get-tuple-element.46, s32[3]{0:T(128)S(1)} %get-tuple-element.45), kind=kLoop, calls=%fused_computation | loop fusion | flops 12 | bytes 73 | tf_op jit(solution)/shard_map/jit(_where)/select_n | solution.py:535
  5.7 7.5 %prologue.1 = (f32[256,1]{1,0:T(8,128)}, bf16[256,8]{1,0:T(8,128)(2,1)}, bf16[256,8]{1,0:T(8,128)(2,1)}, bf16[256,768]{1,0:T(8,128)(2,1)}, bf16[256,384]{1,0:T(8,128)(2,1)}) custom-call(s32[6]{0:T(128)} %broadcast_select_fusion.heads_ref, bf16[256,8192]{1,0:T(8,128)(2,1)} %bitcast.7, bf16[64,128]{1,0:T(8,128)(2,1)} %bitcast.20, bf16[8,8192]{1,0:T(8,128)(2,1)} %qdown_ref.3, ...), custom_call_target="tpu_custom_call" | custom-call | flops 83886080 | bytes 4194304 | tf_op jit(solution)/shard_map/prologue/pallas_call | solution.py:91
  13.2 0.8 %collective-permute-start.1 = (bf16[256,384]{1,0:T(8,128)(2,1)}, bf16[256,384]{1,0:T(8,128)(2,1)S(1)}, u32[]{:S(2)}, u32[]{:S(2)}) collective-permute-start(bf16[256,384]{1,0:T(8,128)(2,1)} %get-tuple-element.29), channel_id=1, source_target_pairs={{24,0},{0,8},{8,16},{16,24},{25,1},{1,9},{9,17},{17,25},{26,2},{2,... | collective-permute-start | bytes 589832 | tf_op jit(solution)/shard_map/ppermute | solution.py:28
  14.0 6.7 %attention.3 = (f32[256,256]{1,0:T(8,128)}, f32[8,2048]{1,0:T(8,128)}, f32[8,256]{1,0:T(8,128)}) custom-call(s32[6]{0:T(128)} %broadcast_select_fusion.heads_ref, bf16[256,6144]{1,0:T(8,128)(2,1)} %bitcast.9, bf16[256,6144]{1,0:T(8,128)(2,1)} %bitcast.12, bf16[256,768]{1,0:T(8,128)(2,1)} %bitcast.17, bf16[256,768]{1,0:T(8,128)(2,1)} %get-tuple-element.26.refs_3_, ...), custom_call_target="tpu_custom_call" | custom-call | flops 3221225472 | bytes 2097152 | tf_op jit(solution)/shard_map/attention/pallas_call | solution.py:231
  20.7 0.0 collective-permute-done.1.refs_8_
  20.8 0.0 copy-start.2
  20.8 0.0 collective-permute-done.refs_7_
  20.8 0.0 copy-start.1
  20.8 0.6 copy-done.2
  21.4 0.1 copy-done.1
  21.6 13.0 %attention.4 = (f32[256,384]{1,0:T(8,128)}, f32[8,3072]{1,0:T(8,128)}, f32[8,256]{1,0:T(8,128)}, bf16[256,384]{1,0:T(8,128)(2,1)}) custom-call(s32[6]{0:T(128)} %broadcast_select_fusion.heads_ref, bf16[256,6144]{1,0:T(8,128)(2,1)} %bitcast.10, bf16[256,6144]{1,0:T(8,128)(2,1)} %bitcast.13, bf16[256,768]{1,0:T(8,128)(2,1)} %bitcast.18, ...), custom_call_target="tpu_custom_call" | custom-call | flops 4831838208 | bytes 3145728 | tf_op jit(solution)/shard_map/attention/pallas_call | solution.py:231
  34.6 2.1 %collective-permute-start.2 = (bf16[256,384]{1,0:T(8,128)(2,1)}, bf16[256,384]{1,0:T(8,128)(2,1)S(1)}, u32[]{:S(2)}, u32[]{:S(2)}) collective-permute-start(bf16[256,384]{1,0:T(8,128)(2,1)} %get-tuple-element.32), channel_id=1, source_target_pairs={{8,0},{16,8},{24,16},{0,24},{9,1},{17,9},{25,17},{1,25},{10,2},{18... | collective-permute-start | bytes 589832 | tf_op jit(solution)/shard_map/ppermute | solution.py:28
  36.7 4.5 %attention.5 = (f32[256,128]{1,0:T(8,128)}, f32[8,1024]{1,0:T(8,128)}, f32[8,256]{1,0:T(8,128)}) custom-call(s32[6]{0:T(128)} %broadcast_select_fusion.heads_ref, bf16[256,6144]{1,0:T(8,128)(2,1)} %bitcast.11, bf16[256,6144]{1,0:T(8,128)(2,1)} %bitcast.14, bf16[256,768]{1,0:T(8,128)(2,1)} %bitcast.19, bf16[256,768]{1,0:T(8,128)(2,1)} %get-tuple-element.26.refs_3_, ...), custom_call_target="tpu_custom_call" | custom-call | flops 1610612736 | bytes 1048576 | tf_op jit(solution)/shard_map/attention/pallas_call | solution.py:231
  41.2 0.1 collective-permute-done.2.handed_ref
  41.3 0.0 copy-start
  41.3 0.7 copy-done
  42.0 8.7 %epilogue.1.packed_ref = bf16[8,24576]{1,0:T(8,128)(2,1)} custom-call(s32[6]{0:T(128)} %broadcast_select_fusion.heads_ref, bf16[256,8192]{1,0:T(8,128)(2,1)} %bitcast.8, f32[256,1]{1,0:T(8,128)} %get-tuple-element.25.inv_ref, bf16[64,128]{1,0:T(8,128)(2,1)} %bitcast.21, bf16[8,8192]{1,0:T(8,128)(2,1)} %qdown_ref.3, bf16[8,8192]{1,0:T(8,128)(2,1)} %vdown_ref.3, ...), custom_call_target="tpu_custom_call" | custom-call | flops 167772160 | bytes 4194304 | tf_op jit(solution)/shard_map/epilogue/pallas_call | solution.py:328
  50.7 22.7 %reduced.1.full_ref = bf16[8,24576]{1,0:T(8,128)(2,1)} custom-call(bf16[8,24576]{1,0:T(8,128)(2,1)} %epilogue.1.packed_ref), custom_call_target="tpu_custom_call" | custom-call | tf_op jit(solution)/shard_map/reduced/pallas_call | solution.py:495
  73.5 2.2 %finished.1 = (f32[8,8192]{1,0:T(8,128)}, f32[8,6144]{1,0:T(8,128)}, f32[8,8192]{1,0:T(8,128)}, f32[8,768]{1,0:T(8,128)}, f32[64,128]{1,0:T(8,128)}) custom-call(bf16[8,24576]{1,0:T(8,128)(2,1)} %reduced.1.full_ref), custom_call_target="tpu_custom_call" | custom-call | tf_op jit(solution)/shard_map/finished/pallas_call | solution.py:377
Async XLA Ops:
  0.6 20.1 %collective-permute-start = (bf16[256,768]{1,0:T(8,128)(2,1)}, bf16[256,768]{1,0:T(8,128)(2,1)S(1)}, u32[]{:S(2)}, u32[]{:S(2)}) collective-permute-start(bf16[256,768]{1,0:T(8,128)(2,1)} %bitcast.16), channel_id=1, source_target_pairs={{24,0},{0,8},{8,16},{16,24},{25,1},{1,9},{9,17},{17,25},{26,2},{2,... | collective-permute-start | bytes 1179656 | tf_op jit(solution)/shard_map/ppermute | solution.py:28
  13.2 7.6 %collective-permute-start.1 = (bf16[256,384]{1,0:T(8,128)(2,1)}, bf16[256,384]{1,0:T(8,128)(2,1)S(1)}, u32[]{:S(2)}, u32[]{:S(2)}) collective-permute-start(bf16[256,384]{1,0:T(8,128)(2,1)} %get-tuple-element.29), channel_id=1, source_target_pairs={{24,0},{0,8},{8,16},{16,24},{25,1},{1,9},{9,17},{17,25},{26,2},{2,... | collective-permute-start | bytes 589832 | tf_op jit(solution)/shard_map/ppermute | solution.py:28
  20.8 0.7 copy-start.2
  20.8 0.8 %copy-start.1 = (bf16[256,768]{1,0:T(8,128)(2,1)}, bf16[256,768]{1,0:T(8,128)(2,1)S(1)}, u32[]{:S(2)}) copy-start(bf16[256,768]{1,0:T(8,128)(2,1)S(1)} %collective-permute-done.refs_7_) | copy-start | bytes 1179652
  34.6 6.8 %collective-permute-start.2 = (bf16[256,384]{1,0:T(8,128)(2,1)}, bf16[256,384]{1,0:T(8,128)(2,1)S(1)}, u32[]{:S(2)}, u32[]{:S(2)}) collective-permute-start(bf16[256,384]{1,0:T(8,128)(2,1)} %get-tuple-element.32), channel_id=1, source_target_pairs={{8,0},{16,8},{24,16},{0,24},{9,1},{17,9},{25,17},{1,25},{10,2},{18... | collective-permute-start | bytes 589832 | tf_op jit(solution)/shard_map/ppermute | solution.py:28
  41.3 0.7 copy-start

commit v4 on v3

--- a/solution.py
+++ b/solution.py
@@ -30,6 +30,12 @@
 
 def dot(left, right, dims):
     return lax.dot_general(left, right, dims, preferred_element_type=F32)
+
+
+def pick(order, slot):
+    count = order.shape[0]
+    shift = lax.rem(lax.axis_index("seq"), 2) * (count // 2)
+    return order[lax.rem(slot + shift, count)]
 
 
 def scaled(block, scale_ref, first, chunks):
@@ -77,7 +83,7 @@
     ).astype(BF16)
     half = given_ref.shape[1] // HEAD_SIZE
     for i in range(half):
-        at = pl.multiple_of(heads_ref[half + i] * HEAD_SIZE, HEAD_SIZE)
+        at = pl.multiple_of(pick(heads_ref, half + i) * HEAD_SIZE, HEAD_SIZE)
         given_ref[:, i * HEAD_SIZE : (i + 1) * HEAD_SIZE] = value_ref[:, pl.ds(at, HEAD_SIZE)]
 
 
@@ -195,7 +201,7 @@
     kv_heads = keys.shape[1] // HEAD_SIZE
     wide = queries // kv_heads
     rank = up.shape[0]
-    by_head = lambda i, heads: (0, heads[first + i])
+    by_head = lambda i, heads: (0, pick(heads, first + i))
     by_slot = lambda i, heads: (0, i)
     whole = lambda i, heads: (0, 0)
     narrow = pl.BlockSpec((rows, HEAD_SIZE), by_head)
@@ -282,7 +288,7 @@
                     other = handed_ref[:, given * HEAD_SIZE : (given + 1) * HEAD_SIZE]
                     dv = dv + other.astype(F32)
                 dv = dv.astype(BF16)
-                head = heads_ref[first + i]
+                head = pick(heads_ref, first + i)
                 at = pl.multiple_of(head * HEAD_SIZE, HEAD_SIZE)
                 dv_mid = dv_mid + dot(vup_ref[:, pl.ds(at, HEAD_SIZE)], dv, NT)
                 at = pl.multiple_of(base + head * HEAD_SIZE, HEAD_SIZE)
@@ -531,8 +537,7 @@
     queries = query_up_weight.shape[1]
     kv = value_up_weight.shape[1]
     half = head_ordering.shape[0] // 2
-    odd = lax.axis_index("seq") % 2 == 1
-    heads = jnp.where(odd, jnp.roll(head_ordering, -half), head_ordering)
+    heads = head_ordering
     scale = norm_scale_vector.reshape(width // LANES, LANES)
     x, fq, grads, keys = layer_input[0], frozen_queries[0], output_gradient[0], frozen_keys[0]
     prior_keys = from_behind(keys, "seq", 1)

time: 76.2 us -> 74 us (0.971)
  other arithmetic: 1.24 us -> 0 us
  local copies, waits for them, and re-layouts: 2.27 us -> 1.48 us
    select_n x1 -> x0, other arithmetic: 1.24 us -> none  [shards(): heads = jnp.where(odd, jnp.roll(head_ordering, -half), head_ordering)]
    slice x1 -> x0, local copies, waits for them, and re-layouts: 0.8 us -> none  [shards(): heads = jnp.where(odd, jnp.roll(head_ordering, -half), head_ordering)]
  transfers between devices with their start and end apart: 3 -> 3, of which waited for: 1 -> 1; matrix products, arithmetic and copies ran while one was open for 3% -> 0% of each run, Pallas kernels for 25% -> 25%
where the time goes in v4:
time: 74 us; the launch traced here: 73.5 us
  Pallas kernels  65 us (88%)
  starting transfers between devices  5.98 us (8%)
  local copies, waits for them, and re-layouts  1.48 us (2%)
    pallas_call x3, Pallas kernels, attention(): pl.pallas_call(functools.partial(attention_kernel, start is not None, pri...  24.1 us
    pallas_call x1, Pallas kernels, reduced(): pl.pallas_call(functools.partial(reduce_kernel, seqs, planes), in_specs=[...  22.5 us
    pallas_call x1, Pallas kernels, epilogue(): pl.pallas_call(functools.partial(epilogue_kernel, counts), grid_spec=pltp...  8.72 us
    pallas_call x1, Pallas kernels, prologue(): pl.pallas_call(prologue_kernel, grid_spec=pltpu.PrefetchScalarGridSpec(nu...  7.47 us
    ppermute x3, starting transfers between devices, from_behind(): return lax.ppermute(block, axis, route)  5.98 us
    pallas_call x1, Pallas kernels, finished(): pl.pallas_call(functools.partial(finish_kernel, limit), in_specs=[vmem],...  2.18 us
  transfers between devices with their start and end apart: 3, of which 1 were waited for; matrix products, arithmetic and copies ran while one was open for 0% of the time, Pallas kernels for 25%

profile of v4, /device:TPU:0, one launch (start us, length us, event | category | flops | bytes accessed | tf_op | source)
XLA Modules:
  0.0 73.5 jit_solution(4246368556655571537)
XLA Ops:
  0.6 3.0 %collective-permute-start = (bf16[256,768]{1,0:T(8,128)(2,1)}, bf16[256,768]{1,0:T(8,128)(2,1)S(1)}, u32[]{:S(2)}, u32[]{:S(2)}) collective-permute-start(bf16[256,768]{1,0:T(8,128)(2,1)} %bitcast.16), channel_id=1, source_target_pairs={{24,0},{0,8},{8,16},{16,24},{25,1},{1,9},{9,17},{17,25},{26,2},{2,... | collective-permute-start | bytes 1179656 | tf_op jit(solution)/shard_map/ppermute | solution.py:28
  3.6 7.5 %prologue.1 = (f32[256,1]{1,0:T(8,128)}, bf16[256,8]{1,0:T(8,128)(2,1)}, bf16[256,8]{1,0:T(8,128)(2,1)}, bf16[256,768]{1,0:T(8,128)(2,1)}, bf16[256,384]{1,0:T(8,128)(2,1)}) custom-call(s32[6]{0:T(128)} %heads_ref.9, bf16[256,8192]{1,0:T(8,128)(2,1)} %bitcast.7, bf16[64,128]{1,0:T(8,128)(2,1)} %bitcast.20, bf16[8,8192]{1,0:T(8,128)(2,1)} %qdown_ref.3, ...), custom_call_target="tpu_custom_call" | custom-call | flops 83886080 | bytes 4194304 | tf_op jit(solution)/shard_map/prologue/pallas_call | solution.py:97
  11.1 1.5 %collective-permute-start.1 = (bf16[256,384]{1,0:T(8,128)(2,1)}, bf16[256,384]{1,0:T(8,128)(2,1)S(1)}, u32[]{:S(2)}, u32[]{:S(2)}) collective-permute-start(bf16[256,384]{1,0:T(8,128)(2,1)} %get-tuple-element.29), channel_id=1, source_target_pairs={{24,0},{0,8},{8,16},{16,24},{25,1},{1,9},{9,17},{17,25},{26,2},{2,... | collective-permute-start | bytes 589832 | tf_op jit(solution)/shard_map/ppermute | solution.py:28
  12.6 6.6 %attention.3 = (f32[256,256]{1,0:T(8,128)}, f32[8,2048]{1,0:T(8,128)}, f32[8,256]{1,0:T(8,128)}) custom-call(s32[6]{0:T(128)} %heads_ref.9, bf16[256,6144]{1,0:T(8,128)(2,1)} %bitcast.9, bf16[256,6144]{1,0:T(8,128)(2,1)} %bitcast.12, bf16[256,768]{1,0:T(8,128)(2,1)} %bitcast.17, bf16[256,768]{1,0:T(8,128)(2,1)} %get-tuple-element.26.refs_3_, ...), custom_call_target="tpu_custom_call" | custom-call | flops 3221225472 | bytes 2097152 | tf_op jit(solution)/shard_map/attention/pallas_call | solution.py:237
  19.2 0.0 collective-permute-done.1.refs_8_
  19.3 0.0 copy-start.2
  19.3 0.0 collective-permute-done.refs_7_
  19.3 0.0 copy-start.1
  19.3 0.6 copy-done.2
  19.9 0.1 copy-done.1
  20.1 13.0 %attention.4 = (f32[256,384]{1,0:T(8,128)}, f32[8,3072]{1,0:T(8,128)}, f32[8,256]{1,0:T(8,128)}, bf16[256,384]{1,0:T(8,128)(2,1)}) custom-call(s32[6]{0:T(128)} %heads_ref.9, bf16[256,6144]{1,0:T(8,128)(2,1)} %bitcast.10, bf16[256,6144]{1,0:T(8,128)(2,1)} %bitcast.13, bf16[256,768]{1,0:T(8,128)(2,1)} %bitcast.18, ...), custom_call_target="tpu_custom_call" | custom-call | flops 4831838208 | bytes 3145728 | tf_op jit(solution)/shard_map/attention/pallas_call | solution.py:237
  33.1 1.5 %collective-permute-start.2 = (bf16[256,384]{1,0:T(8,128)(2,1)}, bf16[256,384]{1,0:T(8,128)(2,1)S(1)}, u32[]{:S(2)}, u32[]{:S(2)}) collective-permute-start(bf16[256,384]{1,0:T(8,128)(2,1)} %get-tuple-element.32), channel_id=1, source_target_pairs={{8,0},{16,8},{24,16},{0,24},{9,1},{17,9},{25,17},{1,25},{10,2},{18... | collective-permute-start | bytes 589832 | tf_op jit(solution)/shard_map/ppermute | solution.py:28
  34.5 4.5 %attention.5 = (f32[256,128]{1,0:T(8,128)}, f32[8,1024]{1,0:T(8,128)}, f32[8,256]{1,0:T(8,128)}) custom-call(s32[6]{0:T(128)} %heads_ref.9, bf16[256,6144]{1,0:T(8,128)(2,1)} %bitcast.11, bf16[256,6144]{1,0:T(8,128)(2,1)} %bitcast.14, bf16[256,768]{1,0:T(8,128)(2,1)} %bitcast.19, bf16[256,768]{1,0:T(8,128)(2,1)} %get-tuple-element.26.refs_3_, ...), custom_call_target="tpu_custom_call" | custom-call | flops 1610612736 | bytes 1048576 | tf_op jit(solution)/shard_map/attention/pallas_call | solution.py:237
  39.0 0.3 collective-permute-done.2.handed_ref
  39.3 0.0 copy-start
  39.4 0.7 copy-done
  40.0 8.7 %epilogue.1.packed_ref = bf16[8,24576]{1,0:T(8,128)(2,1)} custom-call(s32[6]{0:T(128)} %heads_ref.9, bf16[256,8192]{1,0:T(8,128)(2,1)} %bitcast.8, f32[256,1]{1,0:T(8,128)} %get-tuple-element.25.inv_ref, bf16[64,128]{1,0:T(8,128)(2,1)} %bitcast.21, bf16[8,8192]{1,0:T(8,128)(2,1)} %qdown_ref.3, bf16[8,8192]{1,0:T(8,128)(2,1)} %vdown_ref.3, ...), custom_call_target="tpu_custom_call" | custom-call | flops 167772160 | bytes 4194304 | tf_op jit(solution)/shard_map/epilogue/pallas_call | solution.py:334
  48.7 22.5 %reduced.1.full_ref = bf16[8,24576]{1,0:T(8,128)(2,1)} custom-call(bf16[8,24576]{1,0:T(8,128)(2,1)} %epilogue.1.packed_ref), custom_call_target="tpu_custom_call" | custom-call | tf_op jit(solution)/shard_map/reduced/pallas_call | solution.py:501
  71.3 2.2 %finished.1 = (f32[8,8192]{1,0:T(8,128)}, f32[8,6144]{1,0:T(8,128)}, f32[8,8192]{1,0:T(8,128)}, f32[8,768]{1,0:T(8,128)}, f32[64,128]{1,0:T(8,128)}) custom-call(bf16[8,24576]{1,0:T(8,128)(2,1)} %reduced.1.full_ref), custom_call_target="tpu_custom_call" | custom-call | tf_op jit(solution)/shard_map/finished/pallas_call | solution.py:383
Async XLA Ops:
  0.6 18.6 %collective-permute-start = (bf16[256,768]{1,0:T(8,128)(2,1)}, bf16[256,768]{1,0:T(8,128)(2,1)S(1)}, u32[]{:S(2)}, u32[]{:S(2)}) collective-permute-start(bf16[256,768]{1,0:T(8,128)(2,1)} %bitcast.16), channel_id=1, source_target_pairs={{24,0},{0,8},{8,16},{16,24},{25,1},{1,9},{9,17},{17,25},{26,2},{2,... | collective-permute-start | bytes 1179656 | tf_op jit(solution)/shard_map/ppermute | solution.py:28
  11.1 8.1 %collective-permute-start.1 = (bf16[256,384]{1,0:T(8,128)(2,1)}, bf16[256,384]{1,0:T(8,128)(2,1)S(1)}, u32[]{:S(2)}, u32[]{:S(2)}) collective-permute-start(bf16[256,384]{1,0:T(8,128)(2,1)} %get-tuple-element.29), channel_id=1, source_target_pairs={{24,0},{0,8},{8,16},{16,24},{25,1},{1,9},{9,17},{17,25},{26,2},{2,... | collective-permute-start | bytes 589832 | tf_op jit(solution)/shard_map/ppermute | solution.py:28
  19.3 0.7 copy-start.2
  19.3 0.8 %copy-start.1 = (bf16[256,768]{1,0:T(8,128)(2,1)}, bf16[256,768]{1,0:T(8,128)(2,1)S(1)}, u32[]{:S(2)}) copy-start(bf16[256,768]{1,0:T(8,128)(2,1)S(1)} %collective-permute-done.refs_7_) | copy-start | bytes 1179652
  33.1 6.3 %collective-permute-start.2 = (bf16[256,384]{1,0:T(8,128)(2,1)}, bf16[256,384]{1,0:T(8,128)(2,1)S(1)}, u32[]{:S(2)}, u32[]{:S(2)}) collective-permute-start(bf16[256,384]{1,0:T(8,128)(2,1)} %get-tuple-element.32), channel_id=1, source_target_pairs={{8,0},{16,8},{24,16},{0,24},{9,1},{17,9},{25,17},{1,25},{10,2},{18... | collective-permute-start | bytes 589832 | tf_op jit(solution)/shard_map/ppermute | solution.py:28
  39.3 0.7 copy-start
